TPU v7x, 32 devices: a whole 2x2x4 slice. The times are simulated.
32 devices in a mesh: grp: 2 (over x), tm: 16 (over z, y, core).
Axes of the slice: x: 2, y: 2, z: 4, core: 2. Of those that a mesh axis runs over, the one named last changes fastest.
Arguments:
- states: float32 [32, 84, 12, 128], P(('grp', 'tm')), parts along dimension 0, may hold values from -6 to 6
- slab_steps: int32 [32], P(('grp', 'tm')), parts along dimension 0, may hold values from 0 to 999
- offset: int32 [2], P('grp'), parts along dimension 0, may hold values from 0 to 999
- log_sigma: float32 [1000], replicated, may hold values from -2 to 2
- step_size: float32 [1000], replicated, may hold values from -0.12 to -0.03
- w_in: bfloat16 [9, 256, 84], replicated, may hold values from -0.21875 to 0.21875
- w_mid: bfloat16 [9, 256, 256], replicated, may hold values from -0.125 to 0.125
- w_out: bfloat16 [9, 84, 256], replicated, may hold values from -0.125 to 0.125
- embed: float32 [256], replicated, may hold values from -5 to 5
Outputs:
- new_states: float32 [32, 84, 12, 128], P(('grp', 'tm')), parts along dimension 0
There are 2 independent parts, one for each index of `grp`. A program takes and returns all parts, laid end to end along the dimension named above; an argument that names none is the same for every part. Nothing has to cross between parts.
All inputs are finite; a program needn't handle non-finite values.
Results may differ from a plain program's by a relative error of at most 0.0011.
Values sent between devices are 32-bit elements; how exact they have to be, the bound alone decides.
No kernel may reach another device: no remote copies, remote signals or barrier semaphores. Data moves between devices by JAX's collectives and lax.ppermute only.
A program may use at most 64 MiB of HBM per device.

v0:
```python
import jax
import jax.numpy as jnp
from jax import lax
from jax.sharding import PartitionSpec as P

TABLE = 1000
SWEEPS = 2


def convolve(field, weights):
    channels, rows, cols = field.shape
    padded = jnp.pad(field, ((0, 0), (1, 1), (1, 1)))
    total = jnp.zeros((weights.shape[1], rows * cols), jnp.float32)
    for kernel_tap in range(9):
        row_shift = kernel_tap // 3
        col_shift = kernel_tap % 3
        window = padded[:, row_shift : row_shift + rows, col_shift : col_shift + cols].reshape(
            channels, rows * cols
        )
        total = total + jnp.dot(weights[kernel_tap], window, preferred_element_type=jnp.float32)
    return total


def drift_field(field, log_noise, w_in, w_mid, w_out, embed):
    fields, rows, cols = field.shape
    hidden = w_in.shape[1]
    first = convolve(field.astype(jnp.bfloat16), w_in) + log_noise * embed[:, None]
    first = jax.nn.silu(first).astype(jnp.bfloat16).reshape(hidden, rows, cols)
    second = jax.nn.silu(convolve(first, w_mid)).astype(jnp.bfloat16).reshape(hidden, rows, cols)
    return convolve(second, w_out).reshape(fields, rows, cols)


def earlier_sum(increment):
    owners = lax.axis_size("tm")
    flat = increment.reshape(1, -1)
    by_cells = lax.all_to_all(flat, "tm", split_axis=1, concat_axis=0, tiled=True)
    slab_ids = jnp.arange(owners, dtype=jnp.int32)
    lower = (slab_ids[:, None] > slab_ids[None, :]).astype(jnp.float32)
    exclusive = jnp.dot(
        lower, by_cells, precision=lax.Precision.HIGHEST, preferred_element_type=jnp.float32
    )
    back = lax.all_to_all(exclusive, "tm", split_axis=0, concat_axis=1, tiled=True)
    return back.reshape(increment.shape)


def shards(states, slab_steps, offset, log_sigma, step_size, w_in, w_mid, w_out, embed):
    owner = lax.axis_index("tm")
    table_row = (slab_steps[0] + offset[0]) % TABLE
    onehot = jnp.arange(TABLE, dtype=jnp.int32) == table_row
    log_noise = jnp.sum(jnp.where(onehot, log_sigma, 0.0))
    step_len = jnp.sum(jnp.where(onehot, step_size, 0.0))
    field = states[0]
    is_first = owner == 0
    before = field
    increment = field
    for sweep_index in range(SWEEPS):
        increment = step_len * drift_field(field, log_noise, w_in, w_mid, w_out, embed)
        increment = increment + jnp.where(is_first, field, jnp.zeros_like(field))
        before = earlier_sum(increment)
        if sweep_index + 1 < SWEEPS:
            field = jnp.where(is_first, field, before)
    result = before + increment
    return result[None]


def solution(mesh):
    in_specs = (
        P(("grp", "tm"), None, None, None),
        P(("grp", "tm")),
        P("grp"),
        P(),
        P(),
        P(),
        P(),
        P(),
        P(),
    )
    out_specs = P(("grp", "tm"), None, None, None)
    return jax.shard_map(shards, mesh=mesh, in_specs=in_specs, out_specs=out_specs, check_vma=False)
```

profile of v0, /device:TPU:0, one launch (start us, length us, event | category | flops | bytes accessed | tf_op | source)
XLA Modules:
  0.0 143.6 jit_solution(4096677743401641618)
XLA Ops:
  1.3 1.1 copy.120
  2.4 2.4 %convert_reduce_fusion = bf16[84,12,128]{2,1,0:T(8,128)(2,1)S(1)} fusion(f32[1,84,12,128]{3,0,2,1:T(1,128)} %param.9), kind=kLoop, calls=%fused_computation.130 | loop fusion | flops 129024 | bytes 774144 | tf_op jit(solution)/shard_map/convert_element_type | solution.py:27
  4.9 0.8 copy.88
  6.4 0.8 copy.87
  7.3 0.8 copy.85
  8.2 0.8 copy.86
  11.5 1.5 %convolution_bitcast_fusion.3 = f32[256,1536]{0,1:T(8,128)} fusion(bf16[84,1536]{1,0:T(8,128)(2,1)S(1)} %bitcast.384, bf16[9,256,84]{1,2,0:T(8,128)(2,1)S(1)} %copy-done.7), kind=kOutput, calls=%fused_computation.41 | convolution fusion | flops 66060288 | bytes 1888256 | tf_op jit(solution)/shard_map/dot_general | solution.py:20
  13.1 1.6 %convolution_bitcast_fusion.4 = f32[256,1536]{0,1:T(8,128)} fusion(bf16[84,1536]{1,0:T(8,128)(2,1)S(1)} %bitcast.382, bf16[9,256,84]{1,2,0:T(8,128)(2,1)S(1)} %copy-done.7), kind=kOutput, calls=%fused_computation.42 | convolution fusion | flops 66060288 | bytes 1888256 | tf_op jit(solution)/shard_map/dot_general | solution.py:20
  14.6 1.5 %convolution_bitcast_fusion.5 = f32[256,1536]{0,1:T(8,128)} fusion(bf16[84,1536]{1,0:T(8,128)(2,1)S(1)} %bitcast.381, bf16[9,256,84]{1,2,0:T(8,128)(2,1)S(1)} %copy-done.7), kind=kOutput, calls=%fused_computation.43 | convolution fusion | flops 66060288 | bytes 1888256 | tf_op jit(solution)/shard_map/dot_general | solution.py:20
  16.2 1.3 select_reduce_fusion
  17.5 1.3 broadcast_multiply_fusion
  18.8 1.4 convolution_add_fusion.27
  21.7 1.0 copy-done.4
  23.2 1.0 multiply_convert_fusion.3
  24.1 2.3 %pad_slice_fusion.40 = (bf16[256,12,128]{0,2,1:T(8,128)(2,1)S(1)}, bf16[256,12,128]{0,2,1:T(8,128)(2,1)S(1)}, bf16[256,12,128]{0,2,1:T(8,128)(2,1)S(1)}, bf16[25...) fusion(bf16[256,12,128]{0,2,1:T(8,128)(2,1)S(1)} %bitcast.349), kind=kLoop, calls=%fused_computation.111 | loop fusion | bytes 7077888 | tf_op jit(solution)/shard_map/slice | solution.py:17
  30.4 2.1 %pad_slice_fusion.32 = (bf16[256,12,128]{0,2,1:T(8,128)(2,1)S(1)}, bf16[256,12,128]{0,2,1:T(8,128)(2,1)S(1)}, bf16[256,12,128]{0,2,1:T(8,128)(2,1)S(1)}, bf16[25...) fusion(bf16[256,12,128]{0,2,1:T(8,128)(2,1)S(1)} %bitcast.333), kind=kLoop, calls=%fused_computation.103 | loop fusion | bytes 7077888 | tf_op jit(solution)/shard_map/slice | solution.py:17
  35.5 1.0 fusion.12
  37.8 21.4 %all_to_all.52 = f32[1,16,8064]{2,0,1:T(1,128)S(1)} all-to-all(f32[1,16,8064]{2,0,1:T(1,128)S(1)} %fusion.15), channel_id=1, replica_groups=mesh['grp'=2,'tm'=16] {'tm'}, dimensions={1} | all-to-all | bytes 1032192 | tf_op jit(solution)/shard_map/all_to_all | solution.py:36
  60.1 18.1 %all_to_all.53 = f32[16,1,8064]{2,1,0:T(1,128)S(1)} all-to-all(f32[16,1,8064]{2,1,0:T(1,128)S(1)} %copy.67), channel_id=1, replica_groups=mesh['grp'=2,'tm'=16] {'tm'}, dimensions={0} | all-to-all | bytes 1032192 | tf_op jit(solution)/shard_map/all_to_all | solution.py:42
  78.2 1.3 reduce.1
  79.4 1.0 reshape.322
  80.6 1.1 fusion.14
  88.7 2.1 %pad_slice_fusion.24 = (bf16[256,12,128]{0,2,1:T(8,128)(2,1)S(1)}, bf16[256,12,128]{0,2,1:T(8,128)(2,1)S(1)}, bf16[256,12,128]{0,2,1:T(8,128)(2,1)S(1)}, bf16[25...) fusion(bf16[256,12,128]{0,2,1:T(8,128)(2,1)S(1)} %bitcast.350), kind=kLoop, calls=%fused_computation.95 | loop fusion | bytes 7077888 | tf_op jit(solution)/shard_map/slice | solution.py:17
  94.8 2.4 %pad_slice_fusion.16 = (bf16[256,12,128]{0,2,1:T(8,128)(2,1)S(1)}, bf16[256,12,128]{0,2,1:T(8,128)(2,1)S(1)}, bf16[256,12,128]{0,2,1:T(8,128)(2,1)S(1)}, bf16[25...) fusion(bf16[256,12,128]{0,2,1:T(8,128)(2,1)S(1)} %bitcast.335), kind=kLoop, calls=%fused_computation.87 | loop fusion | bytes 7077888 | tf_op jit(solution)/shard_map/slice | solution.py:17
  100.2 0.9 fusion.13
  101.8 0.9 fusion.16
  102.7 18.1 %all_to_all.54 = f32[1,16,8064]{2,0,1:T(1,128)S(1)} all-to-all(f32[1,16,8064]{2,0,1:T(1,128)S(1)} %fusion.16), channel_id=1, replica_groups=mesh['grp'=2,'tm'=16] {'tm'}, dimensions={1} | all-to-all | bytes 1032192 | tf_op jit(solution)/shard_map/all_to_all | solution.py:36
  121.1 1.3 copy.79
  122.4 4.1 %all-to-all-start.3 = ((f32[16,1,8064]{2,1,0:T(1,128)}), f32[16,1,8064]{2,1,0:T(1,128)S(1)}, u32[]{:S(2)}, u32[]{:S(2)}) async-start(f32[16,1,8064]{2,1,0:T(1,128)} %copy.79), calls=%async_computation.3 | async-start | bytes 1032192 | tf_op jit(solution)/shard_map/all_to_all | solution.py:42
  126.7 14.0 %all-to-all-done.3 = f32[16,1,8064]{2,1,0:T(1,128)S(1)} async-done(((f32[16,1,8064]{2,1,0:T(1,128)}), f32[16,1,8064]{2,1,0:T(1,128)S(1)}, u32[]{:S(2)}, u32[]{:S(2)}) %all-to-all-start.3) | async-done | bytes 516128 | tf_op jit(solution)/shard_map/all_to_all | solution.py:42
  140.7 1.3 reduce.3
  142.3 1.3 copy.80
  (133 shorter events, 29.5 us)
Async XLA Ops:
  9.7 1.0 copy-start.7
  13.1 3.1 %copy-start.12 = (f32[1000]{0:T(1024)S(1)}, f32[1000]{0:T(1024)}, u32[]{:S(2)}) copy-start(f32[1000]{0:T(1024)} %param.12) | copy-start | bytes 12004
  18.8 1.4 copy-start.10
  20.2 1.0 copy-start.9
  20.2 1.5 %copy-start.6 = (f32[256,1536]{0,1:T(8,128)S(1)}, f32[256,1536]{0,1:T(8,128)}, u32[]{:S(2)}) copy-start(f32[256,1536]{0,1:T(8,128)} %convolution_bitcast_fusion.5) | copy-start | bytes 4718596
  21.1 1.5 %copy-start.4 = (f32[256,1536]{0,1:T(8,128)S(1)}, f32[256,1536]{0,1:T(8,128)}, u32[]{:S(2)}) copy-start(f32[256,1536]{0,1:T(8,128)} %convolution_bitcast_fusion.3) | copy-start | bytes 4718596
  21.1 2.0 %copy-start.5 = (f32[256,1536]{0,1:T(8,128)S(1)}, f32[256,1536]{0,1:T(8,128)}, u32[]{:S(2)}) copy-start(f32[256,1536]{0,1:T(8,128)} %convolution_bitcast_fusion.4) | copy-start | bytes 4718596
  21.1 2.0 %copy-start.11 = (bf16[11,8,12,128]{3,1,2,0:T(8,128)(2,1)S(1)}, bf16[11,8,12,128]{3,1,2,0:T(8,128)(2,1)}, u32[]{:S(2)}) copy-start(bf16[11,8,12,128]{3,1,2,0:T(8,128)(2,1)} %copy.88) | copy-start | bytes 811012
  24.1 2.3 %copy-start.1 = (bf16[9,256,256]{2,1,0:T(8,128)(2,1)S(1)}, bf16[9,256,256]{2,1,0:T(8,128)(2,1)}, u32[]{:S(2)}) copy-start(bf16[9,256,256]{2,1,0:T(8,128)(2,1)} %param.15) | copy-start | bytes 3538948
  30.4 2.1 %copy-start.2 = (bf16[9,84,256]{2,1,0:T(8,128)(2,1)S(1)}, bf16[9,84,256]{2,1,0:T(8,128)(2,1)}, u32[]{:S(2)}) copy-start(bf16[9,84,256]{2,1,0:T(8,128)(2,1)} %param.16) | copy-start | bytes 1161220
  35.5 1.6 %copy-start = (f32[1,84,12,128]{3,0,2,1:T(1,128)S(1)}, f32[1,84,12,128]{3,0,2,1:T(1,128)}, u32[]{:S(2)}) copy-start(f32[1,84,12,128]{3,0,2,1:T(1,128)} %param.9) | copy-start | bytes 1548292
  83.8 1.0 copy-start.8
  94.8 2.4 %copy-start.3 = (bf16[9,84,256]{2,1,0:T(8,128)(2,1)S(1)}, bf16[9,84,256]{2,1,0:T(8,128)(2,1)}, u32[]{:S(2)}) copy-start(bf16[9,84,256]{2,1,0:T(8,128)(2,1)} %param.16) | copy-start | bytes 1161220
  122.4 18.3 %all-to-all-start.3 = ((f32[16,1,8064]{2,1,0:T(1,128)}), f32[16,1,8064]{2,1,0:T(1,128)S(1)}, u32[]{:S(2)}, u32[]{:S(2)}) async-start(f32[16,1,8064]{2,1,0:T(1,128)} %copy.79), calls=%async_computation.3 | async-start | bytes 1032192 | tf_op jit(solution)/shard_map/all_to_all | solution.py:42
where the time goes:
time: 144 us
  blocking collectives  57.5 us (40%)
  matrix products  28.8 us (20%)
  local copies, waits for them, and re-layouts  26.4 us (18%)
  waiting for transfers between devices  14 us (10%)
  other arithmetic  10.5 us (7%)
  starting transfers between devices  4.12 us (3%)
  between operations  2.25 us (2%)
    all_to_all x2, blocking collectives, earlier_sum(): lax.all_to_all(flat, 'tm', split_axis=1, concat_axis=0, tiled=True)  39.4 us
    dot_general x54, matrix products, convolve(): jnp.dot(weights[kernel_tap], window, preferred_element_type=jnp.float32)  28.1 us
    all_to_all x1, blocking collectives, earlier_sum(): lax.all_to_all(exclusive, 'tm', split_axis=0, concat_axis=1, tiled=True)  18.1 us
    all_to_all x1, waiting for transfers between devices, earlier_sum(): lax.all_to_all(exclusive, 'tm', split_axis=0, concat_axis=1, tiled=True)  14 us
    slice x22, local copies, waits for them, and re-layouts, convolve(): padded[:, row_shift:row_shift + rows, col_shift:col_shift + cols]  10.9 us
    unnamed x63, local copies, waits for them, and re-layouts  9.87 us
    all_to_all x1, starting transfers between devices, earlier_sum(): lax.all_to_all(exclusive, 'tm', split_axis=0, concat_axis=1, tiled=True)  4.12 us
    convert_element_type x2, other arithmetic, drift_field(): field.astype(jnp.bfloat16)  3.47 us
  transfers between devices with their start and end apart: 1, of which 1 were waited for; matrix products, arithmetic and copies ran while one was open for 0% of the time, Pallas kernels for 0%

commit v1 on v0

v1 whole, which is shorter than its diff:
```python
import jax
import jax.numpy as jnp
from jax import lax
from jax.experimental import pallas as pl
from jax.experimental.pallas import tpu as pltpu
from jax.sharding import PartitionSpec as P

SWEEPS = 2


def up(v, m):
    return -(-v // m) * m


def sweep_kernel(dims, x_ref, step_ref, off_ref, owner_ref, ls_ref, h_ref, emb_ref, w1_ref, w2_ref, w3_ref,
                 o_ref, w1s, w3s, xs, u1, u2):
    fields, hidden, rows, cols, table, per = dims
    kin = up(3 * fields, 16)
    mout = up(fields, 16)
    wide = per * cols
    lane = lax.broadcasted_iota(jnp.int32, (1, cols), 1)
    first_col = lane == 0
    last_col = lane == cols - 1

    def right(v):
        return jnp.where(first_col, 0.0, pltpu.roll(v, 1, 1))

    def left(v):
        return jnp.where(last_col, 0.0, pltpu.roll(v, cols - 1, 1))

    total = step_ref[0] + off_ref[0]
    row = jnp.where(total >= table, total - table, total)
    log_noise = ls_ref[row]
    step_len = h_ref[row]
    is_first = owner_ref[0] == 0

    for a in range(3):
        parts = [w1_ref[3 * a + b].astype(jnp.float32) for b in range(3)]
        pad = kin - 3 * fields
        if pad:
            parts.append(jnp.zeros((pad, hidden), jnp.float32))
        w1s[a] = jnp.concatenate(parts, axis=0).astype(jnp.bfloat16)
        for b in range(3):
            w3s[a, b * mout:b * mout + fields, :] = w3_ref[3 * a + b]
            if mout > fields:
                w3s[a, b * mout + fields:(b + 1) * mout, :] = jnp.zeros((mout - fields, hidden), jnp.bfloat16)
    bias = []
    for t in range(hidden // cols):
        e = emb_ref[t:t + 1, :] * log_noise
        bias.append(jnp.broadcast_to(e, (cols, cols)).T)
    bias = jnp.concatenate(bias, axis=0)
    bias = jnp.concatenate([bias] * per, axis=1)

    zx = jnp.zeros((kin, cols), jnp.bfloat16)
    zu = jnp.zeros((hidden, cols), jnp.bfloat16)
    for edge in (0, (rows + 1) * cols):
        xs[:, edge:edge + cols] = zx
        u2[:, edge:edge + cols] = zu
        for b in range(3):
            u1[b, :, edge:edge + cols] = zu

    def load_row(r):
        v = x_ref[pl.ds(r, fields, stride=rows), :]
        parts = [right(v), v, left(v)]
        if kin > 3 * fields:
            parts.append(jnp.zeros((kin - 3 * fields, cols), jnp.float32))
        xs[:, (r + 1) * cols:(r + 2) * cols] = jnp.concatenate(parts, axis=0).astype(jnp.bfloat16)

    def silu(t):
        return t / (1.0 + jnp.exp(-t))

    def conv1(n):
        acc = None
        for a in range(3):
            lo = (n * per + a) * cols
            d = lax.dot_general(w1s[a], xs[:, lo:lo + wide], (((0,), (0,)), ((), ())),
                                preferred_element_type=jnp.float32)
            acc = d if acc is None else acc + d
        u = silu(acc + bias)
        for i in range(per):
            lo = (n * per + i + 1) * cols
            v = u[:, i * cols:(i + 1) * cols]
            u1[0, :, lo:lo + cols] = right(v).astype(jnp.bfloat16)
            u1[1, :, lo:lo + cols] = v.astype(jnp.bfloat16)
            u1[2, :, lo:lo + cols] = left(v).astype(jnp.bfloat16)

    def conv2(n):
        acc = None
        for a in range(3):
            lo = (n * per + a) * cols
            for b in range(3):
                d = jnp.dot(w2_ref[3 * a + b], u1[b, :, lo:lo + wide], preferred_element_type=jnp.float32)
                acc = d if acc is None else acc + d
        lo = (n * per + 1) * cols
        u2[:, lo:lo + wide] = silu(acc).astype(jnp.bfloat16)

    def conv3(n):
        acc = None
        for a in range(3):
            lo = (n * per + a) * cols
            d = jnp.dot(w3s[a], u2[:, lo:lo + wide], preferred_element_type=jnp.float32)
            acc = d if acc is None else acc + d
        for i in range(per):
            y = acc[:, i * cols:(i + 1) * cols]
            out = right(y[:fields]) + y[mout:mout + fields] + left(y[2 * mout:2 * mout + fields])
            r = n * per + i
            own = x_ref[pl.ds(r, fields, stride=rows), :]
            o_ref[pl.ds(r, fields, stride=rows), :] = step_len * out + jnp.where(is_first, own, 0.0)

    blocks = rows // per
    for r in range(rows):
        load_row(r)
    for n in range(blocks + 2):
        if n < blocks:
            conv1(n)
        if 1 <= n < blocks + 1:
            conv2(n - 1)
        if n >= 2:
            conv3(n - 2)


def sweep(x, slab_steps, offset, owner, log_sigma, step_size, embed, w1t, w2, w3, rows, per=2):
    cols = x.shape[1]
    fields = x.shape[0] // rows
    hidden = w2.shape[1]
    table = log_sigma.shape[0]
    kin = up(3 * fields, 16)
    mout = up(fields, 16)
    dims = (fields, hidden, rows, cols, table, per)
    smem = pl.BlockSpec(memory_space=pltpu.SMEM)
    vmem = pl.BlockSpec(memory_space=pltpu.VMEM)
    flops = 2 * rows * cols * 9 * hidden * (2 * fields + hidden)
    return pl.pallas_call(
        lambda *refs: sweep_kernel(dims, *refs),
        out_shape=jax.ShapeDtypeStruct(x.shape, jnp.float32),
        in_specs=[vmem, smem, smem, smem, smem, smem, vmem, vmem, vmem, vmem],
        out_specs=vmem,
        scratch_shapes=[
            pltpu.VMEM((3, kin, hidden), jnp.bfloat16),
            pltpu.VMEM((3, 3 * mout, hidden), jnp.bfloat16),
            pltpu.VMEM((kin, (rows + 2) * cols), jnp.bfloat16),
            pltpu.VMEM((3, hidden, (rows + 2) * cols), jnp.bfloat16),
            pltpu.VMEM((hidden, (rows + 2) * cols), jnp.bfloat16),
        ],
        compiler_params=pltpu.CompilerParams(vmem_limit_bytes=48 << 20),
        cost_estimate=pl.CostEstimate(flops=flops, transcendentals=2 * hidden * rows * cols, bytes_accessed=4 << 20),
        name="sweep",
    )(x, slab_steps, offset, owner, log_sigma, step_size, embed.reshape(-1, cols), w1t, w2, w3)


def partner(axis, step):
    return [(j, j ^ step) for j in range(lax.axis_size(axis))]


def swap(value, step):
    return lax.ppermute(value, "tm", partner("tm", step))


def earlier_sum(increment, owner):
    owners = lax.axis_size("tm")
    length = increment.shape[0]
    half = length // 2
    quarter = up(half // 2, 8)
    core = owner & 1
    side = (owner >> 1) & 1
    mate = swap(increment, 1)
    pair = increment + mate
    mine = core * half + side * (half - quarter)
    theirs = core * half + (1 - side) * (half - quarter)
    own = lax.dynamic_slice_in_dim(pair, mine, quarter, 0)
    got = swap(lax.dynamic_slice_in_dim(pair, theirs, quarter, 0), 2)
    total = own + got
    before = jnp.zeros_like(total)
    step = 4
    while step < owners:
        far = swap(total, step)
        before = before + jnp.where((owner & step) != 0, far, 0.0)
        total = total + far
        step *= 2
    back = swap(before + jnp.where(side == 0, own, 0.0), 2)
    here = before + jnp.where(side == 1, got, 0.0)
    low = jnp.where(side == 0, here, back)
    high = jnp.where(side == 0, back, here)
    part = jnp.concatenate([low[: half - quarter], high], axis=0)
    rest = swap(part, 1)
    full = jnp.where(core == 0, jnp.concatenate([part, rest], axis=0), jnp.concatenate([rest, part], axis=0))
    return full + jnp.where(core == 1, mate, 0.0)


def shards(states, slab_steps, offset, log_sigma, step_size, w_in, w_mid, w_out, embed):
    owner = lax.axis_index("tm")
    _, fields, rows, cols = states.shape
    field = states.reshape(fields * rows, cols)
    where = owner.reshape(1).astype(jnp.int32)
    w1t = w_in.transpose(0, 2, 1)
    for sweep_index in range(SWEEPS):
        increment = sweep(field, slab_steps, offset, where, log_sigma, step_size, embed, w1t, w_mid, w_out, rows)
        before = earlier_sum(increment, owner)
        if sweep_index + 1 < SWEEPS:
            field = jnp.where(owner == 0, field, before)
    return (before + increment).reshape(states.shape)


def solution(mesh):
    in_specs = (
        P(("grp", "tm"), None, None, None),
        P(("grp", "tm")),
        P("grp"),
        P(),
        P(),
        P(),
        P(),
        P(),
        P(),
    )
    out_specs = P(("grp", "tm"), None, None, None)
    return jax.shard_map(shards, mesh=mesh, in_specs=in_specs, out_specs=out_specs, check_vma=False)
```

time: 144 us -> 78.3 us (0.54)
  blocking collectives: 57.5 us -> 0 us
  matrix products: 28.8 us -> 0 us
  waiting for transfers between devices: 14 us -> 38.8 us
  local copies, waits for them, and re-layouts: 26.4 us -> 6.43 us
  Pallas kernels: 0 us -> 13 us
  starting transfers between devices: 4.12 us -> 16 us
  other arithmetic: 10.5 us -> 2.18 us
    all_to_all x3 -> x0, blocking collectives: 57.5 us -> none  [the longest x2 39.4 us: earlier_sum(): lax.all_to_all(flat, 'tm', split_axis=1, concat_axis=0, tiled=True)]
    ppermute x0 -> x12, waiting for transfers between devices: none -> 38.8 us  [swap(): return lax.ppermute(value, 'tm', partner('tm', step))]
    dot_general x56 -> x0, matrix products: 28.8 us -> none  [the longest x54 28.1 us: convolve(): jnp.dot(weights[kernel_tap], window, preferred_element_type=jnp.float32)]
    ppermute x0 -> x12, starting transfers between devices: none -> 16 us  [swap(): return lax.ppermute(value, 'tm', partner('tm', step))]
    all_to_all x1 -> x0, waiting for transfers between devices: 14 us -> none  [earlier_sum(): lax.all_to_all(exclusive, 'tm', split_axis=0, concat_axis=1, tiled=True)]
    pallas_call x0 -> x2, Pallas kernels: none -> 13 us  [sweep(): pl.pallas_call(lambda *refs: sweep_kernel(dims, *refs), out_shape=jax.Sha...]
    slice x22 -> x0, local copies, waits for them, and re-layouts: 10.9 us -> none  [convolve(): padded[:, row_shift:row_shift + rows, col_shift:col_shift + cols]]
    all_to_all x1 -> x0, starting transfers between devices: 4.12 us -> none  [earlier_sum(): lax.all_to_all(exclusive, 'tm', split_axis=0, concat_axis=1, tiled=True)]
  transfers between devices with their start and end apart: 1 -> 12, of which waited for: 1 -> 12; matrix products, arithmetic and copies ran while one was open for 0% -> 0% of each run, Pallas kernels for 0% -> 0%
where the time goes in v1:
time: 78.3 us; the launch traced here: 77.9 us
  waiting for transfers between devices  38.8 us (50%)
  starting transfers between devices  16 us (20%)
  Pallas kernels  13 us (17%)
  local copies, waits for them, and re-layouts  6.43 us (8%)
  other arithmetic  2.18 us (3%)
  between operations  1.52 us (2%)
    ppermute x12, waiting for transfers between devices, swap(): return lax.ppermute(value, 'tm', partner('tm', step))  38.8 us
    ppermute x12, starting transfers between devices, swap(): return lax.ppermute(value, 'tm', partner('tm', step))  16 us
    pallas_call x2, Pallas kernels, sweep(): pl.pallas_call(lambda *refs: sweep_kernel(dims, *refs), out_shape=jax.Sha...  13 us
    unnamed x28, local copies, waits for them, and re-layouts  6.4 us
  transfers between devices with their start and end apart: 12, of which 12 were waited for; matrix products, arithmetic and copies ran while one was open for 0% of the time, Pallas kernels for 0%

profile of v1, /device:TPU:0, one launch (start us, length us, event | category | flops | bytes accessed | tf_op | source)
XLA Modules:
  0.0 77.9 jit_solution(14085743348307525484)
XLA Ops:
  1.3 1.0 %copy-done = f32[1,84,12,128]{3,0,2,1:T(1,128)S(1)} copy-done((f32[1,84,12,128]{3,0,2,1:T(1,128)S(1)}, f32[1,84,12,128]{3,0,2,1:T(1,128)}, u32[]{:S(2)}) %copy-start) | copy-done | bytes 516120
  2.3 1.3 %copy-done.2 = bf16[9,256,256]{2,1,0:T(8,128)(2,1)S(1)} copy-done((bf16[9,256,256]{2,1,0:T(8,128)(2,1)S(1)}, bf16[9,256,256]{2,1,0:T(8,128)(2,1)}, u32[]{:S(2)}) %copy-start.2) | copy-done | bytes 1179672
  3.6 1.0 %copy-done.4 = bf16[9,256,84]{1,2,0:T(8,128)(2,1)S(1)} copy-done((bf16[9,256,84]{1,2,0:T(8,128)(2,1)S(1)}, bf16[9,256,84]{1,2,0:T(8,128)(2,1)}, u32[]{:S(2)}) %copy-start.4) | copy-done | bytes 387096
  4.6 1.0 %copy-done.6 = bf16[9,84,256]{2,1,0:T(8,128)(2,1)S(1)} copy-done((bf16[9,84,256]{2,1,0:T(8,128)(2,1)S(1)}, bf16[9,84,256]{2,1,0:T(8,128)(2,1)}, u32[]{:S(2)}) %copy-start.6) | copy-done | bytes 387096
  5.6 0.7 copy-done.8
  6.3 0.7 copy-done.10
  7.0 0.7 copy-done.12
  7.7 6.5 %sweep.2 = f32[1008,128]{1,0:T(8,128)S(1)} custom-call(f32[1008,128]{1,0:T(8,128)S(1)} %bitcast.5, s32[1]{0:T(128)S(6)} %copy.12.refs_1_, s32[1]{0:T(128)S(6)} %copy.13.refs_2_, s32[1]{0:T(128)} %bitcast.1.refs_3_, f32[1000]{0:T(1024)S(1)} %copy-done.8, f32[1000]{0:T(1024)S(1)} %copy-done.10, f32[2,128]{1,0:T(2,128)S(1)} %bitcast.9, ...), custom_call_target="tpu_custom_call" | custom-call | flops 3001024512 | bytes 4194304 | tf_op jit(solution)/shard_map/sweep/pallas_call | solution.py:133
  14.2 0.6 collective-permute-start
  14.7 1.5 %collective-permute-done = f32[1008,128]{1,0:T(8,128)S(1)} collective-permute-done((f32[1008,128]{1,0:T(8,128)S(1)}, f32[1008,128]{1,0:T(8,128)S(1)}, u32[]{:S(2)}, u32[]{:S(2)}) %collective-permute-start) | collective-permute-done | bytes 516128 | tf_op jit(solution)/shard_map/ppermute | solution.py:156
  16.3 2.9 %collective-permute-start.1 = (f32[256,128]{1,0:T(8,128)S(1)}, f32[256,128]{1,0:T(8,128)S(1)}, u32[]{:S(2)}, u32[]{:S(2)}) collective-permute-start(f32[256,128]{1,0:T(8,128)S(1)} %constant_dynamic-slice_fusion.1), channel_id=1, source_target_pairs={{0,2},{1,3},{2,0},{3,1},{4,6},{5,7},{6,4},{7,5},{8,10},{9,11},{10,... | collective-permute-start | bytes 393224 | tf_op jit(solution)/shard_map/ppermute | solution.py:156
  19.3 3.8 %collective-permute-done.1 = f32[256,128]{1,0:T(8,128)S(1)} collective-permute-done((f32[256,128]{1,0:T(8,128)S(1)}, f32[256,128]{1,0:T(8,128)S(1)}, u32[]{:S(2)}, u32[]{:S(2)}) %collective-permute-start.1) | collective-permute-done | bytes 131104 | tf_op jit(solution)/shard_map/ppermute | solution.py:156
  23.1 1.9 %collective-permute-start.2 = (f32[256,128]{1,0:T(8,128)S(1)}, f32[256,128]{1,0:T(8,128)S(1)}, u32[]{:S(2)}, u32[]{:S(2)}) collective-permute-start(f32[256,128]{1,0:T(8,128)S(1)} %dynamic-slice_add_fusion.1), channel_id=1, source_target_pairs={{0,4},{1,5},{2,6},{3,7},{4,0},{5,1},{6,2},{7,3},{8,12},{9,13},{10,... | collective-permute-start | bytes 393224 | tf_op jit(solution)/shard_map/ppermute | solution.py:156
  24.9 3.2 %collective-permute-done.2 = f32[256,128]{1,0:T(8,128)S(1)} collective-permute-done((f32[256,128]{1,0:T(8,128)S(1)}, f32[256,128]{1,0:T(8,128)S(1)}, u32[]{:S(2)}, u32[]{:S(2)}) %collective-permute-start.2) | collective-permute-done | bytes 131104 | tf_op jit(solution)/shard_map/ppermute | solution.py:156
  28.1 2.9 %collective-permute-start.3 = (f32[256,128]{1,0:T(8,128)S(1)}, f32[256,128]{1,0:T(8,128)S(1)}, u32[]{:S(2)}, u32[]{:S(2)}) collective-permute-start(f32[256,128]{1,0:T(8,128)S(1)} %add.67), channel_id=1, source_target_pairs={{0,8},{1,9},{2,10},{3,11},{4,12},{5,13},{6,14},{7,15},{8,0},{9,1},... | collective-permute-start | bytes 393224 | tf_op jit(solution)/shard_map/ppermute | solution.py:156
  31.0 4.7 %collective-permute-done.3 = f32[256,128]{1,0:T(8,128)S(1)} collective-permute-done((f32[256,128]{1,0:T(8,128)S(1)}, f32[256,128]{1,0:T(8,128)S(1)}, u32[]{:S(2)}, u32[]{:S(2)}) %collective-permute-start.3) | collective-permute-done | bytes 131104 | tf_op jit(solution)/shard_map/ppermute | solution.py:156
  35.8 1.6 %collective-permute-start.4 = (f32[256,128]{1,0:T(8,128)S(1)}, f32[256,128]{1,0:T(8,128)S(1)}, u32[]{:S(2)}, u32[]{:S(2)}) collective-permute-start(f32[256,128]{1,0:T(8,128)S(1)} %select_add_fusion.3), channel_id=1, source_target_pairs={{0,2},{1,3},{2,0},{3,1},{4,6},{5,7},{6,4},{7,5},{8,10},{9,11},{10,... | collective-permute-start | bytes 393224 | tf_op jit(solution)/shard_map/ppermute | solution.py:156
  37.3 3.5 %collective-permute-done.4 = f32[256,128]{1,0:T(8,128)S(1)} collective-permute-done((f32[256,128]{1,0:T(8,128)S(1)}, f32[256,128]{1,0:T(8,128)S(1)}, u32[]{:S(2)}, u32[]{:S(2)}) %collective-permute-start.4) | collective-permute-done | bytes 131104 | tf_op jit(solution)/shard_map/ppermute | solution.py:156
  40.9 0.7 pad_maximum_fusion
  41.7 1.7 %collective-permute-done.5 = f32[504,128]{1,0:T(8,128)S(1)} collective-permute-done((f32[504,128]{1,0:T(8,128)}, f32[504,128]{1,0:T(8,128)S(1)}, u32[]{:S(2)}, u32[]{:S(2)}) %collective-permute-start.5) | collective-permute-done | bytes 258080 | tf_op jit(solution)/shard_map/ppermute | solution.py:156
  43.6 6.5 %sweep.3 = f32[1008,128]{1,0:T(8,128)S(1)} custom-call(f32[1008,128]{1,0:T(8,128)S(1)} %fusion.1.refs_0_, s32[1]{0:T(128)S(6)} %copy.12.refs_1_, s32[1]{0:T(128)S(6)} %copy.13.refs_2_, s32[1]{0:T(128)} %bitcast.1.refs_3_, f32[1000]{0:T(1024)S(1)} %copy-done.9, f32[1000]{0:T(1024)S(1)} %copy-done.11, f32[2,128]{1,0:T(2,128)S(1)} %bitcast.10, ...), custom_call_target="tpu_custom_call" | custom-call | flops 3001024512 | bytes 4194304 | tf_op jit(solution)/shard_map/sweep/pallas_call | solution.py:133
  50.3 1.8 %collective-permute-done.6 = f32[1008,128]{1,0:T(8,128)S(1)} collective-permute-done((f32[1008,128]{1,0:T(8,128)S(1)}, f32[1008,128]{1,0:T(8,128)S(1)}, u32[]{:S(2)}, u32[]{:S(2)}) %collective-permute-start.6) | collective-permute-done | bytes 516128 | tf_op jit(solution)/shard_map/ppermute | solution.py:156
  52.2 1.6 %collective-permute-start.7 = (f32[256,128]{1,0:T(8,128)S(1)}, f32[256,128]{1,0:T(8,128)S(1)}, u32[]{:S(2)}, u32[]{:S(2)}) collective-permute-start(f32[256,128]{1,0:T(8,128)S(1)} %constant_dynamic-slice_fusion), channel_id=1, source_target_pairs={{0,2},{1,3},{2,0},{3,1},{4,6},{5,7},{6,4},{7,5},{8,10},{9,11},{10,... | collective-permute-start | bytes 393224 | tf_op jit(solution)/shard_map/ppermute | solution.py:156
  53.7 4.1 %collective-permute-done.7 = f32[256,128]{1,0:T(8,128)S(1)} collective-permute-done((f32[256,128]{1,0:T(8,128)S(1)}, f32[256,128]{1,0:T(8,128)S(1)}, u32[]{:S(2)}, u32[]{:S(2)}) %collective-permute-start.7) | collective-permute-done | bytes 131104 | tf_op jit(solution)/shard_map/ppermute | solution.py:156
  57.8 0.7 collective-permute-start.8
  58.5 4.3 %collective-permute-done.8 = f32[256,128]{1,0:T(8,128)S(1)} collective-permute-done((f32[256,128]{1,0:T(8,128)S(1)}, f32[256,128]{1,0:T(8,128)S(1)}, u32[]{:S(2)}, u32[]{:S(2)}) %collective-permute-start.8) | collective-permute-done | bytes 131104 | tf_op jit(solution)/shard_map/ppermute | solution.py:156
  62.9 2.1 %collective-permute-start.9 = (f32[256,128]{1,0:T(8,128)S(1)}, f32[256,128]{1,0:T(8,128)S(1)}, u32[]{:S(2)}, u32[]{:S(2)}) collective-permute-start(f32[256,128]{1,0:T(8,128)S(1)} %add.74), channel_id=1, source_target_pairs={{0,8},{1,9},{2,10},{3,11},{4,12},{5,13},{6,14},{7,15},{8,0},{9,1},... | collective-permute-start | bytes 393224 | tf_op jit(solution)/shard_map/ppermute | solution.py:156
  64.9 5.3 %collective-permute-done.9 = f32[256,128]{1,0:T(8,128)S(1)} collective-permute-done((f32[256,128]{1,0:T(8,128)S(1)}, f32[256,128]{1,0:T(8,128)S(1)}, u32[]{:S(2)}, u32[]{:S(2)}) %collective-permute-start.9) | collective-permute-done | bytes 131104 | tf_op jit(solution)/shard_map/ppermute | solution.py:156
  70.2 1.6 %collective-permute-start.10 = (f32[256,128]{1,0:T(8,128)S(1)}, f32[256,128]{1,0:T(8,128)S(1)}, u32[]{:S(2)}, u32[]{:S(2)}) collective-permute-start(f32[256,128]{1,0:T(8,128)S(1)} %select_add_fusion), channel_id=1, source_target_pairs={{0,2},{1,3},{2,0},{3,1},{4,6},{5,7},{6,4},{7,5},{8,10},{9,11},{10,... | collective-permute-start | bytes 393224 | tf_op jit(solution)/shard_map/ppermute | solution.py:156
  71.8 3.5 %collective-permute-done.10 = f32[256,128]{1,0:T(8,128)S(1)} collective-permute-done((f32[256,128]{1,0:T(8,128)S(1)}, f32[256,128]{1,0:T(8,128)S(1)}, u32[]{:S(2)}, u32[]{:S(2)}) %collective-permute-start.10) | collective-permute-done | bytes 131104 | tf_op jit(solution)/shard_map/ppermute | solution.py:156
  75.4 1.5 %collective-permute-done.11 = f32[504,128]{1,0:T(8,128)S(1)} collective-permute-done((f32[504,128]{1,0:T(8,128)S(1)}, f32[504,128]{1,0:T(8,128)S(1)}, u32[]{:S(2)}, u32[]{:S(2)}) %collective-permute-start.11) | collective-permute-done | bytes 258080 | tf_op jit(solution)/shard_map/ppermute | solution.py:156
  76.9 0.9 %fusion.3 = f32[1008,128]{1,0:T(8,128)} fusion(f32[1008,128]{1,0:T(8,128)S(1)} %sweep.3, f32[504,128]{1,0:T(8,128)S(1)} %collective-permute-done.11, f32[256,128]{1,0:T(8,128)S(1)} %get-tuple-element.5, f32[248,128]{1,0:T(8,128)S(1)} %slice_select_fusion, f32[1008,128]{1,0:T(8,128)S(1)} %collective-permute-done.6, pred[]{:T(512)S(6)} %eq.27, pred[]{:T(512)S(6)} %eq.10), kind=kLoop, calls=%fused_computation.5 | loop fusion | flops 1032192 | bytes 2064386 | tf_op jit(solution)/shard_map/add | solution.py:201
  (40 shorter events, 0.9 us)
Async XLA Ops:
  1.3 1.0 %copy-start = (f32[1,84,12,128]{3,0,2,1:T(1,128)S(1)}, f32[1,84,12,128]{3,0,2,1:T(1,128)}, u32[]{:S(2)}) copy-start(f32[1,84,12,128]{3,0,2,1:T(1,128)} %param.9) | copy-start | bytes 1548292
  2.3 1.3 %copy-start.2 = (bf16[9,256,256]{2,1,0:T(8,128)(2,1)S(1)}, bf16[9,256,256]{2,1,0:T(8,128)(2,1)}, u32[]{:S(2)}) copy-start(bf16[9,256,256]{2,1,0:T(8,128)(2,1)} %refs_8_.3) | copy-start | bytes 3538948
  3.6 1.0 %copy-start.4 = (bf16[9,256,84]{1,2,0:T(8,128)(2,1)S(1)}, bf16[9,256,84]{1,2,0:T(8,128)(2,1)}, u32[]{:S(2)}) copy-start(bf16[9,256,84]{1,2,0:T(8,128)(2,1)} %param.14) | copy-start | bytes 1161220
  4.6 1.0 %copy-start.6 = (bf16[9,84,256]{2,1,0:T(8,128)(2,1)S(1)}, bf16[9,84,256]{2,1,0:T(8,128)(2,1)}, u32[]{:S(2)}) copy-start(bf16[9,84,256]{2,1,0:T(8,128)(2,1)} %refs_9_.3) | copy-start | bytes 1161220
  5.6 0.7 copy-start.8
  6.3 0.7 copy-start.10
  7.0 0.7 copy-start.12
  14.2 2.1 %collective-permute-start = (f32[1008,128]{1,0:T(8,128)S(1)}, f32[1008,128]{1,0:T(8,128)S(1)}, u32[]{:S(2)}, u32[]{:S(2)}) collective-permute-start(f32[1008,128]{1,0:T(8,128)S(1)} %sweep.2), channel_id=1, source_target_pairs={{0,1},{1,0},{2,3},{3,2},{4,5},{5,4},{6,7},{7,6},{8,9},{9,8},{10,11... | collective-permute-start | bytes 1548296 | tf_op jit(solution)/shard_map/ppermute | solution.py:156
  16.3 6.7 %collective-permute-start.1 = (f32[256,128]{1,0:T(8,128)S(1)}, f32[256,128]{1,0:T(8,128)S(1)}, u32[]{:S(2)}, u32[]{:S(2)}) collective-permute-start(f32[256,128]{1,0:T(8,128)S(1)} %constant_dynamic-slice_fusion.1), channel_id=1, source_target_pairs={{0,2},{1,3},{2,0},{3,1},{4,6},{5,7},{6,4},{7,5},{8,10},{9,11},{10,... | collective-permute-start | bytes 393224 | tf_op jit(solution)/shard_map/ppermute | solution.py:156
  23.1 5.0 %collective-permute-start.2 = (f32[256,128]{1,0:T(8,128)S(1)}, f32[256,128]{1,0:T(8,128)S(1)}, u32[]{:S(2)}, u32[]{:S(2)}) collective-permute-start(f32[256,128]{1,0:T(8,128)S(1)} %dynamic-slice_add_fusion.1), channel_id=1, source_target_pairs={{0,4},{1,5},{2,6},{3,7},{4,0},{5,1},{6,2},{7,3},{8,12},{9,13},{10,... | collective-permute-start | bytes 393224 | tf_op jit(solution)/shard_map/ppermute | solution.py:156
  28.1 15.3 %copy-start.1 = (f32[1,84,12,128]{3,0,2,1:T(1,128)S(1)}, f32[1,84,12,128]{3,0,2,1:T(1,128)}, u32[]{:S(2)}) copy-start(f32[1,84,12,128]{3,0,2,1:T(1,128)} %param.9) | copy-start | bytes 1548292
  28.1 7.6 %collective-permute-start.3 = (f32[256,128]{1,0:T(8,128)S(1)}, f32[256,128]{1,0:T(8,128)S(1)}, u32[]{:S(2)}, u32[]{:S(2)}) collective-permute-start(f32[256,128]{1,0:T(8,128)S(1)} %add.67), channel_id=1, source_target_pairs={{0,8},{1,9},{2,10},{3,11},{4,12},{5,13},{6,14},{7,15},{8,0},{9,1},... | collective-permute-start | bytes 393224 | tf_op jit(solution)/shard_map/ppermute | solution.py:156
  35.8 5.0 %collective-permute-start.4 = (f32[256,128]{1,0:T(8,128)S(1)}, f32[256,128]{1,0:T(8,128)S(1)}, u32[]{:S(2)}, u32[]{:S(2)}) collective-permute-start(f32[256,128]{1,0:T(8,128)S(1)} %select_add_fusion.3), channel_id=1, source_target_pairs={{0,2},{1,3},{2,0},{3,1},{4,6},{5,7},{6,4},{7,5},{8,10},{9,11},{10,... | collective-permute-start | bytes 393224 | tf_op jit(solution)/shard_map/ppermute | solution.py:156
  40.9 2.7 %copy-start.3 = (bf16[9,256,256]{2,1,0:T(8,128)(2,1)S(1)}, bf16[9,256,256]{2,1,0:T(8,128)(2,1)}, u32[]{:S(2)}) copy-start(bf16[9,256,256]{2,1,0:T(8,128)(2,1)} %refs_8_.3) | copy-start | bytes 3538948
  40.9 2.7 %copy-start.5 = (bf16[9,256,84]{1,2,0:T(8,128)(2,1)S(1)}, bf16[9,256,84]{1,2,0:T(8,128)(2,1)}, u32[]{:S(2)}) copy-start(bf16[9,256,84]{1,2,0:T(8,128)(2,1)} %param.14) | copy-start | bytes 1161220
  40.9 2.7 %copy-start.7 = (bf16[9,84,256]{2,1,0:T(8,128)(2,1)S(1)}, bf16[9,84,256]{2,1,0:T(8,128)(2,1)}, u32[]{:S(2)}) copy-start(bf16[9,84,256]{2,1,0:T(8,128)(2,1)} %refs_9_.3) | copy-start | bytes 1161220
  40.9 2.7 %copy-start.9 = (f32[1000]{0:T(1024)S(1)}, f32[1000]{0:T(1024)}, u32[]{:S(2)}) copy-start(f32[1000]{0:T(1024)} %refs_4_.3) | copy-start | bytes 12004
  40.9 2.7 %copy-start.11 = (f32[1000]{0:T(1024)S(1)}, f32[1000]{0:T(1024)}, u32[]{:S(2)}) copy-start(f32[1000]{0:T(1024)} %refs_5_.3) | copy-start | bytes 12004
  40.9 2.7 %copy-start.13 = (f32[256]{0:T(256)S(1)}, f32[256]{0:T(256)}, u32[]{:S(2)}) copy-start(f32[256]{0:T(256)} %param.17) | copy-start | bytes 3076
  41.7 1.7 %collective-permute-start.5 = (f32[504,128]{1,0:T(8,128)}, f32[504,128]{1,0:T(8,128)S(1)}, u32[]{:S(2)}, u32[]{:S(2)}) collective-permute-start(f32[504,128]{1,0:T(8,128)} %pad_maximum_fusion), channel_id=1, source_target_pairs={{0,1},{1,0},{2,3},{3,2},{4,5},{5,4},{6,7},{7,6},{8,9},{9,8},{10,11... | collective-permute-start | bytes 774152 | tf_op jit(solution)/shard_map/ppermute | solution.py:156
  50.1 2.0 %collective-permute-start.6 = (f32[1008,128]{1,0:T(8,128)S(1)}, f32[1008,128]{1,0:T(8,128)S(1)}, u32[]{:S(2)}, u32[]{:S(2)}) collective-permute-start(f32[1008,128]{1,0:T(8,128)S(1)} %sweep.3), channel_id=1, source_target_pairs={{0,1},{1,0},{2,3},{3,2},{4,5},{5,4},{6,7},{7,6},{8,9},{9,8},{10,11... | collective-permute-start | bytes 1548296 | tf_op jit(solution)/shard_map/ppermute | solution.py:156
  52.2 5.6 %collective-permute-start.7 = (f32[256,128]{1,0:T(8,128)S(1)}, f32[256,128]{1,0:T(8,128)S(1)}, u32[]{:S(2)}, u32[]{:S(2)}) collective-permute-start(f32[256,128]{1,0:T(8,128)S(1)} %constant_dynamic-slice_fusion), channel_id=1, source_target_pairs={{0,2},{1,3},{2,0},{3,1},{4,6},{5,7},{6,4},{7,5},{8,10},{9,11},{10,... | collective-permute-start | bytes 393224 | tf_op jit(solution)/shard_map/ppermute | solution.py:156
  57.8 5.0 %collective-permute-start.8 = (f32[256,128]{1,0:T(8,128)S(1)}, f32[256,128]{1,0:T(8,128)S(1)}, u32[]{:S(2)}, u32[]{:S(2)}) collective-permute-start(f32[256,128]{1,0:T(8,128)S(1)} %dynamic-slice_add_fusion), channel_id=1, source_target_pairs={{0,4},{1,5},{2,6},{3,7},{4,0},{5,1},{6,2},{7,3},{8,12},{9,13},{10,... | collective-permute-start | bytes 393224 | tf_op jit(solution)/shard_map/ppermute | solution.py:156
  62.9 7.3 %collective-permute-start.9 = (f32[256,128]{1,0:T(8,128)S(1)}, f32[256,128]{1,0:T(8,128)S(1)}, u32[]{:S(2)}, u32[]{:S(2)}) collective-permute-start(f32[256,128]{1,0:T(8,128)S(1)} %add.74), channel_id=1, source_target_pairs={{0,8},{1,9},{2,10},{3,11},{4,12},{5,13},{6,14},{7,15},{8,0},{9,1},... | collective-permute-start | bytes 393224 | tf_op jit(solution)/shard_map/ppermute | solution.py:156
  70.2 5.0 %collective-permute-start.10 = (f32[256,128]{1,0:T(8,128)S(1)}, f32[256,128]{1,0:T(8,128)S(1)}, u32[]{:S(2)}, u32[]{:S(2)}) collective-permute-start(f32[256,128]{1,0:T(8,128)S(1)} %select_add_fusion), channel_id=1, source_target_pairs={{0,2},{1,3},{2,0},{3,1},{4,6},{5,7},{6,4},{7,5},{8,10},{9,11},{10,... | collective-permute-start | bytes 393224 | tf_op jit(solution)/shard_map/ppermute | solution.py:156
  75.4 1.6 %collective-permute-start.11 = (f32[504,128]{1,0:T(8,128)S(1)}, f32[504,128]{1,0:T(8,128)S(1)}, u32[]{:S(2)}, u32[]{:S(2)}) collective-permute-start(f32[504,128]{1,0:T(8,128)S(1)} %pad_maximum_fusion.1), channel_id=1, source_target_pairs={{0,1},{1,0},{2,3},{3,2},{4,5},{5,4},{6,7},{7,6},{8,9},{9,8},{10,11... | collective-permute-start | bytes 774152 | tf_op jit(solution)/shard_map/ppermute | solution.py:156

commit v2 on v0

v2 whole, which is shorter than its diff:
```python
import jax
import jax.numpy as jnp
from jax import lax
from jax.experimental import pallas as pl
from jax.experimental.pallas import tpu as pltpu
from jax.sharding import PartitionSpec as P


SWEEPS = 2
BF16 = jnp.bfloat16
F32 = jnp.float32


def up(v, m):
    return -(-v // m) * m


class Sizes:
    def __init__(self, fields, hidden, rows, cols, table):
        self.fields, self.hidden, self.rows, self.cols, self.table = fields, hidden, rows, cols, table
        self.per = 2 if rows % 2 == 0 else 1
        self.blocks = rows // self.per
        self.wide = self.per * cols
        self.kin = up(3 * fields, 16)
        self.mout = up(fields, 16)
        self.cut = (self.blocks + 1) // 2
        self.chunks = ((0, self.cut * self.per), (self.cut * self.per, rows))
        self.long = (rows + 2) * cols


class Body:
    def __init__(self, z, w1s, w2, w3s, bias, par, xs, u1, u2):
        self.z, self.w1s, self.w2, self.w3s, self.bias, self.par = z, w1s, w2, w3s, bias, par
        self.xs, self.u1, self.u2 = xs, u1, u2
        lane = lax.broadcasted_iota(jnp.int32, (1, z.cols), 1)
        self.first_col = lane == 0
        self.last_col = lane == z.cols - 1

    def right(self, v):
        return jnp.where(self.first_col, 0.0, pltpu.roll(v, 1, 1))

    def left(self, v):
        return jnp.where(self.last_col, 0.0, pltpu.roll(v, self.z.cols - 1, 1))

    def clear_edges(self):
        z = self.z
        zx = jnp.zeros((z.kin, z.cols), BF16)
        zu = jnp.zeros((z.hidden, z.cols), BF16)
        for edge in (0, (z.rows + 1) * z.cols):
            self.xs[:, edge:edge + z.cols] = zx
            self.u2[:, edge:edge + z.cols] = zu
            for b in range(3):
                self.u1[b, :, edge:edge + z.cols] = zu

    def load_row(self, r, v):
        z = self.z
        parts = [self.right(v), v, self.left(v)]
        if z.kin > 3 * z.fields:
            parts.append(jnp.zeros((z.kin - 3 * z.fields, z.cols), F32))
        self.xs[:, (r + 1) * z.cols:(r + 2) * z.cols] = jnp.concatenate(parts, axis=0).astype(BF16)

    def silu(self, t):
        return t / (1.0 + jnp.exp(-t))

    def conv1(self, n):
        z = self.z
        acc = None
        for a in range(3):
            lo = (n * z.per + a) * z.cols
            d = lax.dot_general(self.w1s[a], self.xs[:, lo:lo + z.wide], (((0,), (0,)), ((), ())),
                                preferred_element_type=F32)
            acc = d if acc is None else acc + d
        for i in range(z.per):
            lo = (n * z.per + i + 1) * z.cols
            v = self.silu(acc[:, i * z.cols:(i + 1) * z.cols] + self.bias[...])
            self.u1[0, :, lo:lo + z.cols] = self.right(v).astype(BF16)
            self.u1[1, :, lo:lo + z.cols] = v.astype(BF16)
            self.u1[2, :, lo:lo + z.cols] = self.left(v).astype(BF16)

    def conv2(self, n):
        z = self.z
        acc = None
        for a in range(3):
            lo = (n * z.per + a) * z.cols
            for b in range(3):
                d = jnp.dot(self.w2[3 * a + b], self.u1[b, :, lo:lo + z.wide], preferred_element_type=F32)
                acc = d if acc is None else acc + d
        lo = (n * z.per + 1) * z.cols
        self.u2[:, lo:lo + z.wide] = self.silu(acc).astype(BF16)

    def conv3(self, n, emit):
        z = self.z
        acc = None
        for a in range(3):
            lo = (n * z.per + a) * z.cols
            d = jnp.dot(self.w3s[a], self.u2[:, lo:lo + z.wide], preferred_element_type=F32)
            acc = d if acc is None else acc + d
        for i in range(z.per):
            y = acc[:, i * z.cols:(i + 1) * z.cols]
            out = self.right(y[:z.fields]) + y[z.mout:z.mout + z.fields] + self.left(y[2 * z.mout:2 * z.mout + z.fields])
            emit(n * z.per + i, out * self.par[0:1, :])

    def run(self, begin, end, emit, before2=None, before3=None):
        for n in range(self.z.blocks + 2):
            if begin[0] <= n < end[0]:
                self.conv1(n)
            if begin[1] <= n - 1 < end[1]:
                if before2 is not None:
                    before2()
                    before2 = None
                self.conv2(n - 1)
            if begin[2] <= n - 2 < end[2]:
                if before3 is not None:
                    before3()
                    before3 = None
                self.conv3(n - 2, emit)


def own_rows(z, x_ref, r):
    return x_ref[pl.ds(r, z.fields, stride=z.rows), :]


def put_row(z, chunk, out_ref, r, v):
    lo, hi = z.chunks[chunk]
    out_ref[pl.ds(r - lo, z.fields, stride=hi - lo), :] = v


def get_row(z, chunk, in_ref, r):
    lo, hi = z.chunks[chunk]
    return in_ref[pl.ds(r - lo, z.fields, stride=hi - lo), :]


def clip(z, cut):
    return min(cut + 2, z.blocks), min(cut + 1, z.blocks), cut


def open_kernel(z, x_hbm, step_ref, off_ref, owner_ref, place0, place1, place2, place3, ls_hbm, h_hbm, emb_hbm, w1_hbm, w2_hbm, w3_hbm,
                inc_ref, x_ref, w1s, w2v, w3s, bias, par, xs, u1, u2,
                ls_ref, h_ref, emb_ref, w1_ref, w3_ref, sems):
    copies = [pltpu.make_async_copy(src, dst, sems.at[k]) for k, (src, dst) in enumerate([
        (ls_hbm, ls_ref), (h_hbm, h_ref), (emb_hbm, emb_ref), (x_hbm, x_ref), (w1_hbm, w1_ref),
        (w2_hbm, w2v), (w3_hbm, w3_ref)])]
    for copy in copies:
        copy.start()
    body = Body(z, w1s, w2v, w3s, bias, par, xs, u1, u2)
    body.clear_edges()
    for copy in copies[:3]:
        copy.wait()
    total = step_ref[0] + off_ref[0]
    row = jnp.where(total >= z.table, total - z.table, total)
    log_noise = ls_ref[row]
    par[0:1, :] = jnp.full((1, z.cols), h_ref[row], F32)
    par[1:2, :] = jnp.where(owner_ref[0] == 0, jnp.ones((1, z.cols), F32), jnp.zeros((1, z.cols), F32))
    for t in range(z.hidden // z.cols):
        e = emb_ref[t:t + 1, :] * log_noise
        bias[t * z.cols:(t + 1) * z.cols, :] = jnp.broadcast_to(e, (z.cols, z.cols)).T
    copies[3].wait()
    for r in range(z.rows):
        body.load_row(r, own_rows(z, x_ref, r))
    copies[4].wait()
    for a in range(3):
        parts = [w1_ref[3 * a + b].astype(F32) for b in range(3)]
        if z.kin > 3 * z.fields:
            parts.append(jnp.zeros((z.kin - 3 * z.fields, z.hidden), F32))
        w1s[a] = jnp.concatenate(parts, axis=0).astype(BF16)

    def before3():
        copies[6].wait()
        for a in range(3):
            for b in range(3):
                w3s[a, b * z.mout:b * z.mout + z.fields, :] = w3_ref[3 * a + b]
                if z.mout > z.fields:
                    w3s[a, b * z.mout + z.fields:(b + 1) * z.mout, :] = jnp.zeros((z.mout - z.fields, z.hidden), BF16)

    is_first = par[1:2, :] > 0.0

    def emit(r, v):
        put_row(z, 0, inc_ref, r, v + jnp.where(is_first, own_rows(z, x_ref, r), 0.0))

    body.run((0, 0, 0), clip(z, z.cut), emit, copies[5].wait, before3)


def close_kernel(z, x_ref, w1s, w2, w3s, bias, par, xs_in, u1_in, u2_in, inc_ref, xs, u1, u2):
    body = Body(z, w1s, w2, w3s, bias, par, xs, u1, u2)
    is_first = par[1:2, :] > 0.0

    def emit(r, v):
        put_row(z, 1, inc_ref, r, v + jnp.where(is_first, own_rows(z, x_ref, r), 0.0))

    body.run(clip(z, z.cut), (z.blocks,) * 3, emit)


def later_kernel(z, x_ref, f0_ref, f1_ref, w1s, w2_hbm, w3s, bias, par, inc_ref, w2, xs, u1, u2, sem):
    copy = pltpu.make_async_copy(w2_hbm, w2, sem)
    copy.start()
    body = Body(z, w1s, w2, w3s, bias, par, xs, u1, u2)
    body.clear_edges()
    is_first = par[1:2, :] > 0.0
    for chunk, ref in enumerate((f0_ref, f1_ref)):
        for r in range(*z.chunks[chunk]):
            body.load_row(r, jnp.where(is_first, own_rows(z, x_ref, r), get_row(z, chunk, ref, r)))

    def emit(r, v):
        put_row(z, 0, inc_ref, r, v + jnp.where(is_first, own_rows(z, x_ref, r), 0.0))

    body.run((0, 0, 0), clip(z, z.cut), emit, copy.wait)


def merge_kernel(z, a_ref, b_ref, o_ref):
    for chunk, ref in enumerate((a_ref, b_ref)):
        for r in range(*z.chunks[chunk]):
            o_ref[pl.ds(r, z.fields, stride=z.rows), :] = get_row(z, chunk, ref, r)


VMEM = pl.BlockSpec(memory_space=pltpu.VMEM)
SMEM = pl.BlockSpec(memory_space=pltpu.SMEM)
HBM = pl.BlockSpec(memory_space=pltpu.HBM)


def shape(*dims, dtype=F32):
    return jax.ShapeDtypeStruct(dims, dtype)


def params():
    return pltpu.CompilerParams(vmem_limit_bytes=20 << 20)


def cost(z, share):
    flops = int(share * 2 * z.rows * z.cols * 9 * z.hidden * (2 * z.fields + z.hidden))
    return pl.CostEstimate(flops=flops, transcendentals=int(share * 2 * z.hidden * z.rows * z.cols), bytes_accessed=1 << 20)


class Program:
    def __init__(self, z):
        self.z = z
        self.state = [shape(z.kin, z.long, dtype=BF16), shape(3, z.hidden, z.long, dtype=BF16), shape(z.hidden, z.long, dtype=BF16)]

    def chunk_shape(self, chunk):
        lo, hi = self.z.chunks[chunk]
        return shape(self.z.fields * (hi - lo), self.z.cols)

    def open(self, x, slab_steps, offset, owner, places, log_sigma, step_size, embed, w1t, w2, w3):
        z = self.z
        outs = [self.chunk_shape(0), shape(*x.shape), shape(3, z.kin, z.hidden, dtype=BF16), shape(*w2.shape, dtype=BF16),
                shape(3, 3 * z.mout, z.hidden, dtype=BF16), shape(z.hidden, z.cols), shape(8, z.cols)] + self.state
        far = [pltpu.with_memory_space_constraint(v, pltpu.HBM) for v in (log_sigma, step_size, embed, w1t, w2, w3)]
        res = pl.pallas_call(
            lambda *refs: open_kernel(z, *refs), out_shape=outs,
            in_specs=[HBM, SMEM, SMEM, SMEM] + [SMEM] * 4 + [HBM] * 6, out_specs=[VMEM] * len(outs),
            scratch_shapes=[pltpu.SMEM((z.table,), F32), pltpu.SMEM((z.table,), F32), pltpu.VMEM(embed.shape, F32),
                            pltpu.VMEM(w1t.shape, BF16), pltpu.VMEM(w3.shape, BF16), pltpu.SemaphoreType.DMA((7,))],
            compiler_params=params(), cost_estimate=cost(z, 0.7), name="open",
        )(pltpu.with_memory_space_constraint(x, pltpu.HBM), slab_steps, offset, owner, *[v.reshape(1) for v in places], *far)
        self.w2 = res[3]
        self.fixed = list(res[2:7])
        self.x = res[1]
        return res[0], list(res[7:])

    def close(self, state):
        z = self.z
        ins = [self.x, *self.fixed, *state]
        outs = [self.chunk_shape(1)] + self.state
        res = pl.pallas_call(
            lambda *refs: close_kernel(z, *refs), out_shape=outs, in_specs=[VMEM] * len(ins), out_specs=[VMEM] * len(outs),
            input_output_aliases={len(ins) - 3 + k: 1 + k for k in range(3)},
            compiler_params=params(), cost_estimate=cost(z, 0.3), name="close",
        )(*ins)
        return res[0]

    def later(self, x, w2, sum0, sum1):
        z = self.z
        self.x = x
        self.fixed[1] = pltpu.with_memory_space_constraint(w2, pltpu.HBM)
        ins = [x, sum0, sum1, *self.fixed]
        outs = [self.chunk_shape(0), shape(*w2.shape, dtype=BF16)] + self.state
        specs = [VMEM] * 4 + [HBM] + [VMEM] * 3
        res = pl.pallas_call(
            lambda *refs: later_kernel(z, *refs), out_shape=outs, in_specs=specs, out_specs=[VMEM] * len(outs),
            scratch_shapes=[pltpu.SemaphoreType.DMA],
            compiler_params=params(), cost_estimate=cost(z, 0.7), name="later",
        )(*ins)
        self.fixed[1] = res[1]
        return res[0], list(res[2:])

    def merge(self, a, b):
        z = self.z
        return pl.pallas_call(
            lambda *refs: merge_kernel(z, *refs), out_shape=shape(z.fields * z.rows, z.cols),
            in_specs=[VMEM, VMEM], out_specs=VMEM, compiler_params=params(), name="merge",
        )(a, b)


def swap(value, step):
    return lax.ppermute(value, "tm", [(j, j ^ step) for j in range(lax.axis_size("tm"))])


def places_of(owner, length):
    half = up(length // 2, 8)
    quarter = up(half // 2, 8)
    base = (owner & 1) * (length - half)
    side = (owner >> 1) & 1
    return base + side * (half - quarter), base + (1 - side) * (half - quarter)


def earlier_sum(increment, owner, places):
    owners = lax.axis_size("tm")
    length = increment.shape[0]
    half = up(length // 2, 8)
    quarter = up(half // 2, 8)
    core = owner & 1
    side = (owner >> 1) & 1
    mate = swap(increment, 1)
    pair = increment + mate
    own = lax.dynamic_slice(pair, (places[0], 0), (quarter, pair.shape[1]), allow_negative_indices=False)
    theirs = lax.dynamic_slice(pair, (places[1], 0), (quarter, pair.shape[1]), allow_negative_indices=False)
    got = swap(theirs, 2)
    total = own + got
    before = jnp.zeros_like(total)
    for k in range(2, owners.bit_length() - 1):
        far = swap(total, 1 << k)
        before = before + jnp.where((owner & (1 << k)) != 0, far, 0.0)
        total = total + far
    back = swap(before + jnp.where(side == 0, own, 0.0), 2)
    here = before + jnp.where(side == 1, got, 0.0)
    low = jnp.where(side == 0, here, back)
    high = jnp.where(side == 0, back, here)
    part = jnp.concatenate([low[: half - quarter], high], axis=0)
    rest = swap(part, 1)
    low = jnp.where(core == 0, part, rest)
    high = jnp.where(core == 0, rest, part)
    full = jnp.concatenate([low[: length - half], high], axis=0)
    return full + jnp.where(core == 1, mate, 0.0)


def shards(states, slab_steps, offset, log_sigma, step_size, w_in, w_mid, w_out, embed):
    owner = lax.axis_index("tm")
    _, fields, rows, cols = states.shape
    z = Sizes(fields, w_in.shape[1], rows, cols, log_sigma.shape[0])
    program = Program(z)
    where = owner.reshape(1).astype(jnp.int32)
    x = states.reshape(fields * rows, cols)
    places = [places_of(owner, fields * (hi - lo)) for lo, hi in z.chunks]
    for sweep_index in range(SWEEPS):
        if sweep_index == 0:
            inc0, state = program.open(x, slab_steps, offset, where, (*places[0], *places[1]), log_sigma, step_size, embed.reshape(-1, cols),
                                       w_in.transpose(0, 2, 1), w_mid, w_out)
        else:
            inc0, state = program.later(x, w_mid, sum0, sum1)
        inc1 = program.close(state)
        sum0 = earlier_sum(inc0, owner, places[0])
        sum1 = earlier_sum(inc1, owner, places[1])
    return program.merge(sum0 + inc0, sum1 + inc1).reshape(states.shape)


def solution(mesh):
    in_specs = (
        P(("grp", "tm"), None, None, None),
        P(("grp", "tm")),
        P("grp"),
        P(),
        P(),
        P(),
        P(),
        P(),
        P(),
    )
    out_specs = P(("grp", "tm"), None, None, None)
    return jax.shard_map(shards, mesh=mesh, in_specs=in_specs, out_specs=out_specs, check_vma=False)
```

time: 144 us -> 66.7 us (0.46)
  blocking collectives: 57.5 us -> 0 us
  matrix products: 28.8 us -> 0 us
  local copies, waits for them, and re-layouts: 26.4 us -> 0.06 us
  starting transfers between devices: 4.12 us -> 28.3 us
  Pallas kernels: 0 us -> 15 us
  other arithmetic: 10.5 us -> 0.7 us
  waiting for transfers between devices: 14 us -> 20.9 us
    all_to_all x3 -> x0, blocking collectives: 57.5 us -> none  [the longest x2 39.4 us: earlier_sum(): lax.all_to_all(flat, 'tm', split_axis=1, concat_axis=0, tiled=True)]
    dot_general x56 -> x0, matrix products: 28.8 us -> none  [the longest x54 28.1 us: convolve(): jnp.dot(weights[kernel_tap], window, preferred_element_type=jnp.float32)]
    ppermute x0 -> x24, starting transfers between devices: none -> 28.3 us  [swap(): lax.ppermute(value, 'tm', [(j, j ^ step) for j in range(lax.axis_size('tm...]
    ppermute x0 -> x24, waiting for transfers between devices: none -> 20.9 us  [swap(): lax.ppermute(value, 'tm', [(j, j ^ step) for j in range(lax.axis_size('tm...]
    pallas_call x0 -> x5, Pallas kernels: none -> 15 us  [the longest x1 5.26 us: open(): pl.pallas_call(lambda *refs: open_kernel(z, *refs), out_shape=outs, in_sp...]
    all_to_all x1 -> x0, waiting for transfers between devices: 14 us -> none  [earlier_sum(): lax.all_to_all(exclusive, 'tm', split_axis=0, concat_axis=1, tiled=True)]
    slice x22 -> x0, local copies, waits for them, and re-layouts: 10.9 us -> none  [convolve(): padded[:, row_shift:row_shift + rows, col_shift:col_shift + cols]]
    unnamed x63 -> x2, local copies, waits for them, and re-layouts: 9.87 us -> 0.01 us
  transfers between devices with their start and end apart: 1 -> 24, of which waited for: 1 -> 18; matrix products, arithmetic and copies ran while one was open for 0% -> 1% of each run, Pallas kernels for 0% -> 0%
where the time goes in v2:
time: 66.7 us; the launch traced here: 66.5 us
  starting transfers between devices  28.3 us (42%)
  waiting for transfers between devices  20.9 us (31%)
  Pallas kernels  15 us (22%)
  between operations  1.58 us (2%)
  other arithmetic  0.7 us (1%)
    ppermute x24, starting transfers between devices, swap(): lax.ppermute(value, 'tm', [(j, j ^ step) for j in range(lax.axis_size('tm...  28.3 us
    ppermute x24, waiting for transfers between devices, swap(): lax.ppermute(value, 'tm', [(j, j ^ step) for j in range(lax.axis_size('tm...  20.9 us
    pallas_call x1, Pallas kernels, open(): pl.pallas_call(lambda *refs: open_kernel(z, *refs), out_shape=outs, in_sp...  5.26 us
    pallas_call x2, Pallas kernels, close(): pl.pallas_call(lambda *refs: close_kernel(z, *refs), out_shape=outs, in_s...  4.48 us
    pallas_call x1, Pallas kernels, later(): pl.pallas_call(lambda *refs: later_kernel(z, *refs), out_shape=outs, in_s...  4.37 us
  transfers between devices with their start and end apart: 24, of which 18 were waited for; matrix products, arithmetic and copies ran while one was open for 1% of the time, Pallas kernels for 0%

profile of v2, /device:TPU:0, one launch (start us, length us, event | category | flops | bytes accessed | tf_op | source)
XLA Modules:
  0.0 66.5 jit_solution(17507138821579151923)
XLA Ops:
  1.3 5.3 %open.1 = (f32[504,128]{1,0:T(8,128)S(1)}, f32[1008,128]{1,0:T(8,128)S(1)}, bf16[3,256,256]{2,1,0:T(8,128)(2,1)S(1)}, bf16[9,256,256]{2,1,0:T(8,128)(2,1)S(1)}, ...) custom-call(f32[1008,128]{1,0:T(8,128)} %bitcast.7, ...), custom_call_target="tpu_custom_call" | custom-call | flops 2100717184 | bytes 1048576 | tf_op jit(solution)/shard_map/open/pallas_call | solution.py:247
  6.6 2.2 %close.2 = (f32[504,128]{1,0:T(8,128)S(1)}, bf16[256,1792]{1,0:T(8,128)(2,1)S(1)}, bf16[3,256,1792]{2,1,0:T(8,128)(2,1)S(1)}, bf16[256,1792]{1,0:T(8,128)(2,1)S(1)}) custom-call(f32[1008,128]{1,0:T(8,128)S(1)} %get-tuple-element.23.refs_0_, ...), custom_call_target="tpu_custom_call", output_to_operand_aliasing={{1}: (6, {}), {2}: (7, {}), {3}: (8, {})} | custom-call | flops 900307328 | bytes 1048576 | tf_op jit(solution)/shard_map/close/pallas_call | solution.py:263
  9.4 1.1 %collective-permute-done.6 = f32[504,128]{1,0:T(8,128)S(1)} collective-permute-done((f32[504,128]{1,0:T(8,128)S(1)}, f32[504,128]{1,0:T(8,128)S(1)}, u32[]{:S(2)}, u32[]{:S(2)}) %collective-permute-start.6) | collective-permute-done | bytes 258080 | tf_op jit(solution)/shard_map/ppermute | solution.py:294
  10.6 2.9 %collective-permute-start.7 = (f32[128,128]{1,0:T(8,128)S(1)}, f32[128,128]{1,0:T(8,128)S(1)}, u32[]{:S(2)}, u32[]{:S(2)}) collective-permute-start(f32[128,128]{1,0:T(8,128)S(1)} %constant_dynamic-slice_fusion.2), channel_id=1, source_target_pairs={{0,2},{1,3},{2,0},{3,1},{4,6},{5,7},{6,4},{7,5},{8,10},{9,11},{10,... | collective-permute-start | bytes 196616 | tf_op jit(solution)/shard_map/ppermute | solution.py:294
  13.9 2.0 %collective-permute-done.7 = f32[128,128]{1,0:T(8,128)S(1)} collective-permute-done((f32[128,128]{1,0:T(8,128)S(1)}, f32[128,128]{1,0:T(8,128)S(1)}, u32[]{:S(2)}, u32[]{:S(2)}) %collective-permute-start.7) | collective-permute-done | bytes 65568 | tf_op jit(solution)/shard_map/ppermute | solution.py:294
  15.9 2.2 %collective-permute-start.8 = (f32[128,128]{1,0:T(8,128)S(1)}, f32[128,128]{1,0:T(8,128)S(1)}, u32[]{:S(2)}, u32[]{:S(2)}) collective-permute-start(f32[128,128]{1,0:T(8,128)S(1)} %dynamic-slice_add_fusion.2), channel_id=1, source_target_pairs={{0,4},{1,5},{2,6},{3,7},{4,0},{5,1},{6,2},{7,3},{8,12},{9,13},{10,... | collective-permute-start | bytes 196616 | tf_op jit(solution)/shard_map/ppermute | solution.py:294
  18.1 1.5 %collective-permute-start.2 = (f32[128,128]{1,0:T(8,128)S(1)}, f32[128,128]{1,0:T(8,128)S(1)}, u32[]{:S(2)}, u32[]{:S(2)}) collective-permute-start(f32[128,128]{1,0:T(8,128)S(1)} %dynamic-slice_add_fusion.3), channel_id=1, source_target_pairs={{0,4},{1,5},{2,6},{3,7},{4,0},{5,1},{6,2},{7,3},{8,12},{9,13},{10,... | collective-permute-start | bytes 196616 | tf_op jit(solution)/shard_map/ppermute | solution.py:294
  19.6 1.2 %collective-permute-done.8 = f32[128,128]{1,0:T(8,128)S(1)} collective-permute-done((f32[128,128]{1,0:T(8,128)S(1)}, f32[128,128]{1,0:T(8,128)S(1)}, u32[]{:S(2)}, u32[]{:S(2)}) %collective-permute-start.8) | collective-permute-done | bytes 65568 | tf_op jit(solution)/shard_map/ppermute | solution.py:294
  20.7 2.8 %collective-permute-start.9 = (f32[128,128]{1,0:T(8,128)S(1)}, f32[128,128]{1,0:T(8,128)S(1)}, u32[]{:S(2)}, u32[]{:S(2)}) collective-permute-start(f32[128,128]{1,0:T(8,128)S(1)} %add.109), channel_id=1, source_target_pairs={{0,8},{1,9},{2,10},{3,11},{4,12},{5,13},{6,14},{7,15},{8,0},{9,1},... | collective-permute-start | bytes 196616 | tf_op jit(solution)/shard_map/ppermute | solution.py:294
  23.5 1.6 %collective-permute-start.3 = (f32[128,128]{1,0:T(8,128)S(1)}, f32[128,128]{1,0:T(8,128)S(1)}, u32[]{:S(2)}, u32[]{:S(2)}) collective-permute-start(f32[128,128]{1,0:T(8,128)S(1)} %add.102), channel_id=1, source_target_pairs={{0,8},{1,9},{2,10},{3,11},{4,12},{5,13},{6,14},{7,15},{8,0},{9,1},... | collective-permute-start | bytes 196616 | tf_op jit(solution)/shard_map/ppermute | solution.py:294
  25.1 2.2 %collective-permute-done.9 = f32[128,128]{1,0:T(8,128)S(1)} collective-permute-done((f32[128,128]{1,0:T(8,128)S(1)}, f32[128,128]{1,0:T(8,128)S(1)}, u32[]{:S(2)}, u32[]{:S(2)}) %collective-permute-start.9) | collective-permute-done | bytes 65568 | tf_op jit(solution)/shard_map/ppermute | solution.py:294
  27.4 1.1 %collective-permute-start.10 = (f32[128,128]{1,0:T(8,128)S(1)}, f32[128,128]{1,0:T(8,128)S(1)}, u32[]{:S(2)}, u32[]{:S(2)}) collective-permute-start(f32[128,128]{1,0:T(8,128)S(1)} %get-tuple-element.43), channel_id=1, source_target_pairs={{0,2},{1,3},{2,0},{3,1},{4,6},{5,7},{6,4},{7,5},{8,10},{9,11},{10,... | collective-permute-start | bytes 196616 | tf_op jit(solution)/shard_map/ppermute | solution.py:294
  28.8 2.1 %collective-permute-start.4 = (f32[128,128]{1,0:T(8,128)S(1)}, f32[128,128]{1,0:T(8,128)S(1)}, u32[]{:S(2)}, u32[]{:S(2)}) collective-permute-start(f32[128,128]{1,0:T(8,128)S(1)} %get-tuple-element.45), channel_id=1, source_target_pairs={{0,2},{1,3},{2,0},{3,1},{4,6},{5,7},{6,4},{7,5},{8,10},{9,11},{10,... | collective-permute-start | bytes 196616 | tf_op jit(solution)/shard_map/ppermute | solution.py:294
  31.8 1.3 %collective-permute-done.4 = f32[128,128]{1,0:T(8,128)S(1)} collective-permute-done((f32[128,128]{1,0:T(8,128)S(1)}, f32[128,128]{1,0:T(8,128)S(1)}, u32[]{:S(2)}, u32[]{:S(2)}) %collective-permute-start.4) | collective-permute-done | bytes 65568 | tf_op jit(solution)/shard_map/ppermute | solution.py:294
  33.3 1.3 %collective-permute-done.5 = f32[256,128]{1,0:T(8,128)S(1)} collective-permute-done((f32[256,128]{1,0:T(8,128)S(1)}, f32[256,128]{1,0:T(8,128)S(1)}, u32[]{:S(2)}, u32[]{:S(2)}) %collective-permute-start.5) | collective-permute-done | bytes 131104 | tf_op jit(solution)/shard_map/ppermute | solution.py:294
  34.7 4.4 %later.1 = (f32[504,128]{1,0:T(8,128)S(1)}, bf16[9,256,256]{2,1,0:T(8,128)(2,1)S(1)}, bf16[256,1792]{1,0:T(8,128)(2,1)S(1)}, bf16[3,256,1792]{2,1,0:T(8,128)(2,1)S(1)}, bf16[256,1792]{1,0:T(8,128)(2,1)S(1)}) custom-call(f32[1008,128]{1,0:T(8,128)S(1)} %bitcast.8, f32[504,128]{1,0:T(8,128)S(1)} %maximum_add_fusion.refs_1_, ...), custom_call_target="tpu_custom_call" | custom-call | flops 2100717184 | bytes 1048576 | tf_op jit(solution)/shard_map/later/pallas_call | solution.py:277
  39.1 2.2 %close.3 = (f32[504,128]{1,0:T(8,128)S(1)}, bf16[256,1792]{1,0:T(8,128)(2,1)S(1)}, bf16[3,256,1792]{2,1,0:T(8,128)(2,1)S(1)}, bf16[256,1792]{1,0:T(8,128)(2,1)S(1)}) custom-call(f32[1008,128]{1,0:T(8,128)S(1)} %bitcast.9, bf16[3,256,256]{2,1,0:T(8,128)(2,1)S(1)} %get-tuple-element.24.refs_1_.refs_3_, ...), custom_call_target="tpu_custom_call", output_to_operand_aliasing={{1}: (6, {}), {2}: (7, {}), {3}: (8, {})} | custom-call | flops 900307328 | bytes 1048576 | tf_op jit(solution)/shard_map/close/pallas_call | solution.py:263
  41.9 1.0 %collective-permute-done.18 = f32[504,128]{1,0:T(8,128)S(1)} collective-permute-done((f32[504,128]{1,0:T(8,128)S(1)}, f32[504,128]{1,0:T(8,128)S(1)}, u32[]{:S(2)}, u32[]{:S(2)}) %collective-permute-start.18) | collective-permute-done | bytes 258080 | tf_op jit(solution)/shard_map/ppermute | solution.py:294
  43.0 2.1 %collective-permute-start.19 = (f32[128,128]{1,0:T(8,128)S(1)}, f32[128,128]{1,0:T(8,128)S(1)}, u32[]{:S(2)}, u32[]{:S(2)}) collective-permute-start(f32[128,128]{1,0:T(8,128)S(1)} %constant_dynamic-slice_fusion), channel_id=1, source_target_pairs={{0,2},{1,3},{2,0},{3,1},{4,6},{5,7},{6,4},{7,5},{8,10},{9,11},{10,... | collective-permute-start | bytes 196616 | tf_op jit(solution)/shard_map/ppermute | solution.py:294
  45.4 2.0 %collective-permute-done.19 = f32[128,128]{1,0:T(8,128)S(1)} collective-permute-done((f32[128,128]{1,0:T(8,128)S(1)}, f32[128,128]{1,0:T(8,128)S(1)}, u32[]{:S(2)}, u32[]{:S(2)}) %collective-permute-start.19) | collective-permute-done | bytes 65568 | tf_op jit(solution)/shard_map/ppermute | solution.py:294
  47.5 1.5 %collective-permute-start.20 = (f32[128,128]{1,0:T(8,128)S(1)}, f32[128,128]{1,0:T(8,128)S(1)}, u32[]{:S(2)}, u32[]{:S(2)}) collective-permute-start(f32[128,128]{1,0:T(8,128)S(1)} %dynamic-slice_add_fusion), channel_id=1, source_target_pairs={{0,4},{1,5},{2,6},{3,7},{4,0},{5,1},{6,2},{7,3},{8,12},{9,13},{10,... | collective-permute-start | bytes 196616 | tf_op jit(solution)/shard_map/ppermute | solution.py:294
  49.5 1.5 %collective-permute-start.14 = (f32[128,128]{1,0:T(8,128)S(1)}, f32[128,128]{1,0:T(8,128)S(1)}, u32[]{:S(2)}, u32[]{:S(2)}) collective-permute-start(f32[128,128]{1,0:T(8,128)S(1)} %dynamic-slice_add_fusion.1), channel_id=1, source_target_pairs={{0,4},{1,5},{2,6},{3,7},{4,0},{5,1},{6,2},{7,3},{8,12},{9,13},{10,... | collective-permute-start | bytes 196616 | tf_op jit(solution)/shard_map/ppermute | solution.py:294
  51.0 1.3 %collective-permute-done.20 = f32[128,128]{1,0:T(8,128)S(1)} collective-permute-done((f32[128,128]{1,0:T(8,128)S(1)}, f32[128,128]{1,0:T(8,128)S(1)}, u32[]{:S(2)}, u32[]{:S(2)}) %collective-permute-start.20) | collective-permute-done | bytes 65568 | tf_op jit(solution)/shard_map/ppermute | solution.py:294
  52.3 2.1 %collective-permute-start.21 = (f32[128,128]{1,0:T(8,128)S(1)}, f32[128,128]{1,0:T(8,128)S(1)}, u32[]{:S(2)}, u32[]{:S(2)}) collective-permute-start(f32[128,128]{1,0:T(8,128)S(1)} %add.124), channel_id=1, source_target_pairs={{0,8},{1,9},{2,10},{3,11},{4,12},{5,13},{6,14},{7,15},{8,0},{9,1},... | collective-permute-start | bytes 196616 | tf_op jit(solution)/shard_map/ppermute | solution.py:294
  54.4 1.9 %collective-permute-start.15 = (f32[128,128]{1,0:T(8,128)S(1)}, f32[128,128]{1,0:T(8,128)S(1)}, u32[]{:S(2)}, u32[]{:S(2)}) collective-permute-start(f32[128,128]{1,0:T(8,128)S(1)} %add.116), channel_id=1, source_target_pairs={{0,8},{1,9},{2,10},{3,11},{4,12},{5,13},{6,14},{7,15},{8,0},{9,1},... | collective-permute-start | bytes 196616 | tf_op jit(solution)/shard_map/ppermute | solution.py:294
  56.3 2.3 %collective-permute-done.21 = f32[128,128]{1,0:T(8,128)S(1)} collective-permute-done((f32[128,128]{1,0:T(8,128)S(1)}, f32[128,128]{1,0:T(8,128)S(1)}, u32[]{:S(2)}, u32[]{:S(2)}) %collective-permute-start.21) | collective-permute-done | bytes 65568 | tf_op jit(solution)/shard_map/ppermute | solution.py:294
  58.7 0.9 %collective-permute-start.22 = (f32[128,128]{1,0:T(8,128)S(1)}, f32[128,128]{1,0:T(8,128)S(1)}, u32[]{:S(2)}, u32[]{:S(2)}) collective-permute-start(f32[128,128]{1,0:T(8,128)S(1)} %get-tuple-element.39), channel_id=1, source_target_pairs={{0,2},{1,3},{2,0},{3,1},{4,6},{5,7},{6,4},{7,5},{8,10},{9,11},{10,... | collective-permute-start | bytes 196616 | tf_op jit(solution)/shard_map/ppermute | solution.py:294
  59.7 2.1 %collective-permute-start.16 = (f32[128,128]{1,0:T(8,128)S(1)}, f32[128,128]{1,0:T(8,128)S(1)}, u32[]{:S(2)}, u32[]{:S(2)}) collective-permute-start(f32[128,128]{1,0:T(8,128)S(1)} %get-tuple-element.41), channel_id=1, source_target_pairs={{0,2},{1,3},{2,0},{3,1},{4,6},{5,7},{6,4},{7,5},{8,10},{9,11},{10,... | collective-permute-start | bytes 196616 | tf_op jit(solution)/shard_map/ppermute | solution.py:294
  61.8 1.2 %collective-permute-done.22 = f32[128,128]{1,0:T(8,128)S(1)} collective-permute-done((f32[128,128]{1,0:T(8,128)S(1)}, f32[128,128]{1,0:T(8,128)S(1)}, u32[]{:S(2)}, u32[]{:S(2)}) %collective-permute-start.22) | collective-permute-done | bytes 65568 | tf_op jit(solution)/shard_map/ppermute | solution.py:294
  63.1 0.9 %collective-permute-done.16 = f32[128,128]{1,0:T(8,128)S(1)} collective-permute-done((f32[128,128]{1,0:T(8,128)S(1)}, f32[128,128]{1,0:T(8,128)S(1)}, u32[]{:S(2)}, u32[]{:S(2)}) %collective-permute-start.16) | collective-permute-done | bytes 65568 | tf_op jit(solution)/shard_map/ppermute | solution.py:294
  64.5 1.0 %collective-permute-done.17 = f32[256,128]{1,0:T(8,128)S(1)} collective-permute-done((f32[256,128]{1,0:T(8,128)S(1)}, f32[256,128]{1,0:T(8,128)S(1)}, u32[]{:S(2)}, u32[]{:S(2)}) %collective-permute-start.17) | collective-permute-done | bytes 131104 | tf_op jit(solution)/shard_map/ppermute | solution.py:294
  65.6 0.8 %merge.1 = f32[1008,128]{1,0:T(8,128)} custom-call(f32[504,128]{1,0:T(8,128)S(1)} %fusion.refs_0_, f32[504,128]{1,0:T(8,128)S(1)} %fusion.1.refs_1_), custom_call_target="tpu_custom_call" | custom-call | tf_op jit(solution)/shard_map/merge/pallas_call | solution.py:287
  (63 shorter events, 4.9 us)
Async XLA Ops:
  8.8 1.7 %collective-permute-start.6 = (f32[504,128]{1,0:T(8,128)S(1)}, f32[504,128]{1,0:T(8,128)S(1)}, u32[]{:S(2)}, u32[]{:S(2)}) collective-permute-start(f32[504,128]{1,0:T(8,128)S(1)} %get-tuple-element.32), channel_id=1, source_target_pairs={{0,1},{1,0},{2,3},{3,2},{4,5},{5,4},{6,7},{7,6},{8,9},{9,8},{10,11... | collective-permute-start | bytes 774152 | tf_op jit(solution)/shard_map/ppermute | solution.py:294
  9.4 4.1 %collective-permute-start = (f32[504,128]{1,0:T(8,128)S(1)}, f32[504,128]{1,0:T(8,128)S(1)}, u32[]{:S(2)}, u32[]{:S(2)}) collective-permute-start(f32[504,128]{1,0:T(8,128)S(1)} %get-tuple-element.22), channel_id=1, source_target_pairs={{0,1},{1,0},{2,3},{3,2},{4,5},{5,4},{6,7},{7,6},{8,9},{9,8},{10,11... | collective-permute-start | bytes 774152 | tf_op jit(solution)/shard_map/ppermute | solution.py:294
  10.6 5.3 %collective-permute-start.7 = (f32[128,128]{1,0:T(8,128)S(1)}, f32[128,128]{1,0:T(8,128)S(1)}, u32[]{:S(2)}, u32[]{:S(2)}) collective-permute-start(f32[128,128]{1,0:T(8,128)S(1)} %constant_dynamic-slice_fusion.2), channel_id=1, source_target_pairs={{0,2},{1,3},{2,0},{3,1},{4,6},{5,7},{6,4},{7,5},{8,10},{9,11},{10,... | collective-permute-start | bytes 196616 | tf_op jit(solution)/shard_map/ppermute | solution.py:294
  13.6 4.5 %collective-permute-start.1 = (f32[128,128]{1,0:T(8,128)S(1)}, f32[128,128]{1,0:T(8,128)S(1)}, u32[]{:S(2)}, u32[]{:S(2)}) collective-permute-start(f32[128,128]{1,0:T(8,128)S(1)} %constant_dynamic-slice_fusion.3), channel_id=1, source_target_pairs={{0,2},{1,3},{2,0},{3,1},{4,6},{5,7},{6,4},{7,5},{8,10},{9,11},{10,... | collective-permute-start | bytes 196616 | tf_op jit(solution)/shard_map/ppermute | solution.py:294
  15.9 18.8 %copy-start = (f32[1,84,12,128]{3,0,2,1:T(1,128)S(1)}, f32[1,84,12,128]{3,0,2,1:T(1,128)}, u32[]{:S(2)}) copy-start(f32[1,84,12,128]{3,0,2,1:T(1,128)} %param.9) | copy-start | bytes 1548292
  15.9 4.8 %collective-permute-start.8 = (f32[128,128]{1,0:T(8,128)S(1)}, f32[128,128]{1,0:T(8,128)S(1)}, u32[]{:S(2)}, u32[]{:S(2)}) collective-permute-start(f32[128,128]{1,0:T(8,128)S(1)} %dynamic-slice_add_fusion.2), channel_id=1, source_target_pairs={{0,4},{1,5},{2,6},{3,7},{4,0},{5,1},{6,2},{7,3},{8,12},{9,13},{10,... | collective-permute-start | bytes 196616 | tf_op jit(solution)/shard_map/ppermute | solution.py:294
  18.1 5.4 %collective-permute-start.2 = (f32[128,128]{1,0:T(8,128)S(1)}, f32[128,128]{1,0:T(8,128)S(1)}, u32[]{:S(2)}, u32[]{:S(2)}) collective-permute-start(f32[128,128]{1,0:T(8,128)S(1)} %dynamic-slice_add_fusion.3), channel_id=1, source_target_pairs={{0,4},{1,5},{2,6},{3,7},{4,0},{5,1},{6,2},{7,3},{8,12},{9,13},{10,... | collective-permute-start | bytes 196616 | tf_op jit(solution)/shard_map/ppermute | solution.py:294
  20.7 6.6 %collective-permute-start.9 = (f32[128,128]{1,0:T(8,128)S(1)}, f32[128,128]{1,0:T(8,128)S(1)}, u32[]{:S(2)}, u32[]{:S(2)}) collective-permute-start(f32[128,128]{1,0:T(8,128)S(1)} %add.109), channel_id=1, source_target_pairs={{0,8},{1,9},{2,10},{3,11},{4,12},{5,13},{6,14},{7,15},{8,0},{9,1},... | collective-permute-start | bytes 196616 | tf_op jit(solution)/shard_map/ppermute | solution.py:294
  23.5 5.2 %collective-permute-start.3 = (f32[128,128]{1,0:T(8,128)S(1)}, f32[128,128]{1,0:T(8,128)S(1)}, u32[]{:S(2)}, u32[]{:S(2)}) collective-permute-start(f32[128,128]{1,0:T(8,128)S(1)} %add.102), channel_id=1, source_target_pairs={{0,8},{1,9},{2,10},{3,11},{4,12},{5,13},{6,14},{7,15},{8,0},{9,1},... | collective-permute-start | bytes 196616 | tf_op jit(solution)/shard_map/ppermute | solution.py:294
  27.4 4.3 %collective-permute-start.10 = (f32[128,128]{1,0:T(8,128)S(1)}, f32[128,128]{1,0:T(8,128)S(1)}, u32[]{:S(2)}, u32[]{:S(2)}) collective-permute-start(f32[128,128]{1,0:T(8,128)S(1)} %get-tuple-element.43), channel_id=1, source_target_pairs={{0,2},{1,3},{2,0},{3,1},{4,6},{5,7},{6,4},{7,5},{8,10},{9,11},{10,... | collective-permute-start | bytes 196616 | tf_op jit(solution)/shard_map/ppermute | solution.py:294
  28.8 4.3 %collective-permute-start.4 = (f32[128,128]{1,0:T(8,128)S(1)}, f32[128,128]{1,0:T(8,128)S(1)}, u32[]{:S(2)}, u32[]{:S(2)}) collective-permute-start(f32[128,128]{1,0:T(8,128)S(1)} %get-tuple-element.45), channel_id=1, source_target_pairs={{0,2},{1,3},{2,0},{3,1},{4,6},{5,7},{6,4},{7,5},{8,10},{9,11},{10,... | collective-permute-start | bytes 196616 | tf_op jit(solution)/shard_map/ppermute | solution.py:294
  31.8 1.5 %collective-permute-start.11 = (f32[256,128]{1,0:T(8,128)S(1)}, f32[256,128]{1,0:T(8,128)S(1)}, u32[]{:S(2)}, u32[]{:S(2)}) collective-permute-start(f32[256,128]{1,0:T(8,128)S(1)} %pad_maximum_fusion.1), channel_id=1, source_target_pairs={{0,1},{1,0},{2,3},{3,2},{4,5},{5,4},{6,7},{7,6},{8,9},{9,8},{10,11... | collective-permute-start | bytes 393224 | tf_op jit(solution)/shard_map/ppermute | solution.py:294
  33.2 1.4 %collective-permute-start.5 = (f32[256,128]{1,0:T(8,128)S(1)}, f32[256,128]{1,0:T(8,128)S(1)}, u32[]{:S(2)}, u32[]{:S(2)}) collective-permute-start(f32[256,128]{1,0:T(8,128)S(1)} %pad_maximum_fusion), channel_id=1, source_target_pairs={{0,1},{1,0},{2,3},{3,2},{4,5},{5,4},{6,7},{7,6},{8,9},{9,8},{10,11... | collective-permute-start | bytes 393224 | tf_op jit(solution)/shard_map/ppermute | solution.py:294
  41.3 1.6 %collective-permute-start.18 = (f32[504,128]{1,0:T(8,128)S(1)}, f32[504,128]{1,0:T(8,128)S(1)}, u32[]{:S(2)}, u32[]{:S(2)}) collective-permute-start(f32[504,128]{1,0:T(8,128)S(1)} %get-tuple-element.38), channel_id=1, source_target_pairs={{0,1},{1,0},{2,3},{3,2},{4,5},{5,4},{6,7},{7,6},{8,9},{9,8},{10,11... | collective-permute-start | bytes 774152 | tf_op jit(solution)/shard_map/ppermute | solution.py:294
  41.6 3.5 %collective-permute-start.12 = (f32[504,128]{1,0:T(8,128)S(1)}, f32[504,128]{1,0:T(8,128)S(1)}, u32[]{:S(2)}, u32[]{:S(2)}) collective-permute-start(f32[504,128]{1,0:T(8,128)S(1)} %get-tuple-element.33), channel_id=1, source_target_pairs={{0,1},{1,0},{2,3},{3,2},{4,5},{5,4},{6,7},{7,6},{8,9},{9,8},{10,11... | collective-permute-start | bytes 774152 | tf_op jit(solution)/shard_map/ppermute | solution.py:294
  43.0 4.5 %collective-permute-start.19 = (f32[128,128]{1,0:T(8,128)S(1)}, f32[128,128]{1,0:T(8,128)S(1)}, u32[]{:S(2)}, u32[]{:S(2)}) collective-permute-start(f32[128,128]{1,0:T(8,128)S(1)} %constant_dynamic-slice_fusion), channel_id=1, source_target_pairs={{0,2},{1,3},{2,0},{3,1},{4,6},{5,7},{6,4},{7,5},{8,10},{9,11},{10,... | collective-permute-start | bytes 196616 | tf_op jit(solution)/shard_map/ppermute | solution.py:294
  45.1 4.3 %collective-permute-start.13 = (f32[128,128]{1,0:T(8,128)S(1)}, f32[128,128]{1,0:T(8,128)S(1)}, u32[]{:S(2)}, u32[]{:S(2)}) collective-permute-start(f32[128,128]{1,0:T(8,128)S(1)} %constant_dynamic-slice_fusion.1), channel_id=1, source_target_pairs={{0,2},{1,3},{2,0},{3,1},{4,6},{5,7},{6,4},{7,5},{8,10},{9,11},{10,... | collective-permute-start | bytes 196616 | tf_op jit(solution)/shard_map/ppermute | solution.py:294
  47.5 4.8 %collective-permute-start.20 = (f32[128,128]{1,0:T(8,128)S(1)}, f32[128,128]{1,0:T(8,128)S(1)}, u32[]{:S(2)}, u32[]{:S(2)}) collective-permute-start(f32[128,128]{1,0:T(8,128)S(1)} %dynamic-slice_add_fusion), channel_id=1, source_target_pairs={{0,4},{1,5},{2,6},{3,7},{4,0},{5,1},{6,2},{7,3},{8,12},{9,13},{10,... | collective-permute-start | bytes 196616 | tf_op jit(solution)/shard_map/ppermute | solution.py:294
  49.5 4.9 %collective-permute-start.14 = (f32[128,128]{1,0:T(8,128)S(1)}, f32[128,128]{1,0:T(8,128)S(1)}, u32[]{:S(2)}, u32[]{:S(2)}) collective-permute-start(f32[128,128]{1,0:T(8,128)S(1)} %dynamic-slice_add_fusion.1), channel_id=1, source_target_pairs={{0,4},{1,5},{2,6},{3,7},{4,0},{5,1},{6,2},{7,3},{8,12},{9,13},{10,... | collective-permute-start | bytes 196616 | tf_op jit(solution)/shard_map/ppermute | solution.py:294
  52.3 6.4 %collective-permute-start.21 = (f32[128,128]{1,0:T(8,128)S(1)}, f32[128,128]{1,0:T(8,128)S(1)}, u32[]{:S(2)}, u32[]{:S(2)}) collective-permute-start(f32[128,128]{1,0:T(8,128)S(1)} %add.124), channel_id=1, source_target_pairs={{0,8},{1,9},{2,10},{3,11},{4,12},{5,13},{6,14},{7,15},{8,0},{9,1},... | collective-permute-start | bytes 196616 | tf_op jit(solution)/shard_map/ppermute | solution.py:294
  54.4 5.2 %collective-permute-start.15 = (f32[128,128]{1,0:T(8,128)S(1)}, f32[128,128]{1,0:T(8,128)S(1)}, u32[]{:S(2)}, u32[]{:S(2)}) collective-permute-start(f32[128,128]{1,0:T(8,128)S(1)} %add.116), channel_id=1, source_target_pairs={{0,8},{1,9},{2,10},{3,11},{4,12},{5,13},{6,14},{7,15},{8,0},{9,1},... | collective-permute-start | bytes 196616 | tf_op jit(solution)/shard_map/ppermute | solution.py:294
  58.7 4.3 %collective-permute-start.22 = (f32[128,128]{1,0:T(8,128)S(1)}, f32[128,128]{1,0:T(8,128)S(1)}, u32[]{:S(2)}, u32[]{:S(2)}) collective-permute-start(f32[128,128]{1,0:T(8,128)S(1)} %get-tuple-element.39), channel_id=1, source_target_pairs={{0,2},{1,3},{2,0},{3,1},{4,6},{5,7},{6,4},{7,5},{8,10},{9,11},{10,... | collective-permute-start | bytes 196616 | tf_op jit(solution)/shard_map/ppermute | solution.py:294
  59.7 4.4 %collective-permute-start.16 = (f32[128,128]{1,0:T(8,128)S(1)}, f32[128,128]{1,0:T(8,128)S(1)}, u32[]{:S(2)}, u32[]{:S(2)}) collective-permute-start(f32[128,128]{1,0:T(8,128)S(1)} %get-tuple-element.41), channel_id=1, source_target_pairs={{0,2},{1,3},{2,0},{3,1},{4,6},{5,7},{6,4},{7,5},{8,10},{9,11},{10,... | collective-permute-start | bytes 196616 | tf_op jit(solution)/shard_map/ppermute | solution.py:294
  63.0 1.4 %collective-permute-start.23 = (f32[256,128]{1,0:T(8,128)S(1)}, f32[256,128]{1,0:T(8,128)S(1)}, u32[]{:S(2)}, u32[]{:S(2)}) collective-permute-start(f32[256,128]{1,0:T(8,128)S(1)} %pad_maximum_fusion.3), channel_id=1, source_target_pairs={{0,1},{1,0},{2,3},{3,2},{4,5},{5,4},{6,7},{7,6},{8,9},{9,8},{10,11... | collective-permute-start | bytes 393224 | tf_op jit(solution)/shard_map/ppermute | solution.py:294
  64.1 1.4 %collective-permute-start.17 = (f32[256,128]{1,0:T(8,128)S(1)}, f32[256,128]{1,0:T(8,128)S(1)}, u32[]{:S(2)}, u32[]{:S(2)}) collective-permute-start(f32[256,128]{1,0:T(8,128)S(1)} %pad_maximum_fusion.2), channel_id=1, source_target_pairs={{0,1},{1,0},{2,3},{3,2},{4,5},{5,4},{6,7},{7,6},{8,9},{9,8},{10,11... | collective-permute-start | bytes 393224 | tf_op jit(solution)/shard_map/ppermute | solution.py:294

commit v3 on v2

--- a/solution.py
+++ b/solution.py
@@ -151,6 +151,7 @@
     log_noise = ls_ref[row]
     par[0:1, :] = jnp.full((1, z.cols), h_ref[row], F32)
     par[1:2, :] = jnp.where(owner_ref[0] == 0, jnp.ones((1, z.cols), F32), jnp.zeros((1, z.cols), F32))
+    par[2:3, :] = jnp.where(owner_ref[0] % 2 == 1, jnp.ones((1, z.cols), F32), jnp.zeros((1, z.cols), F32))
     for t in range(z.hidden // z.cols):
         e = emb_ref[t:t + 1, :] * log_noise
         bias[t * z.cols:(t + 1) * z.cols, :] = jnp.broadcast_to(e, (z.cols, z.cols)).T
@@ -190,26 +191,76 @@
     body.run(clip(z, z.cut), (z.blocks,) * 3, emit)
 
 
-def later_kernel(z, x_ref, f0_ref, f1_ref, w1s, w2_hbm, w3s, bias, par, inc_ref, w2, xs, u1, u2, sem):
+def early(z):
+    return max(z.cut - 1, 0), max(z.cut - 2, 0), 0
+
+
+def assemble(f_ref, part, rest, mate, par, inc=None):
+    length, half = f_ref.shape[0], part.shape[0]
+    cut = length - half
+    odd = par[2:3, :] > 0.0
+    extra = jnp.where(odd, mate[...], 0.0)
+    if inc is not None:
+        extra = extra + inc[...]
+    a, b = part[...], rest[...]
+    f_ref[:cut, :] = jnp.where(odd, b[:cut], a[:cut]) + extra[:cut]
+    f_ref[cut:, :] = jnp.where(odd, a, b) + extra[cut:]
+
+
+def early_kernel(z, x_ref, part, rest, mate, w1s, w2_hbm, bias, par, w2, xs, u1, u2, f_ref, sem):
     copy = pltpu.make_async_copy(w2_hbm, w2, sem)
     copy.start()
+    body = Body(z, w1s, w2, None, bias, par, xs, u1, u2)
+    body.clear_edges()
+    assemble(f_ref, part, rest, mate, par)
+    is_first = par[1:2, :] > 0.0
+    for r in range(*z.chunks[0]):
+        body.load_row(r, jnp.where(is_first, own_rows(z, x_ref, r), get_row(z, 0, f_ref, r)))
+    ends = early(z)
+    body.run((0, 0, 0), (ends[0], 0, 0), None)
+    copy.wait()
+    body.run((ends[0], 0, 0), ends, None)
+
+
+def later_kernel(z, x_ref, part, rest, mate, w1s, w2, w3s, bias, par, xs_in, u1_in, u2_in, inc_ref, xs, u1, u2, f_ref):
     body = Body(z, w1s, w2, w3s, bias, par, xs, u1, u2)
-    body.clear_edges()
+    assemble(f_ref, part, rest, mate, par)
     is_first = par[1:2, :] > 0.0
-    for chunk, ref in enumerate((f0_ref, f1_ref)):
-        for r in range(*z.chunks[chunk]):
-            body.load_row(r, jnp.where(is_first, own_rows(z, x_ref, r), get_row(z, chunk, ref, r)))
+    for r in range(*z.chunks[1]):
+        body.load_row(r, jnp.where(is_first, own_rows(z, x_ref, r), get_row(z, 1, f_ref, r)))
 
     def emit(r, v):
         put_row(z, 0, inc_ref, r, v + jnp.where(is_first, own_rows(z, x_ref, r), 0.0))
 
-    body.run((0, 0, 0), clip(z, z.cut), emit, copy.wait)
-
-
-def merge_kernel(z, a_ref, b_ref, o_ref):
-    for chunk, ref in enumerate((a_ref, b_ref)):
-        for r in range(*z.chunks[chunk]):
-            o_ref[pl.ds(r, z.fields, stride=z.rows), :] = get_row(z, chunk, ref, r)
+    body.run(early(z), clip(z, z.cut), emit)
+
+
+def groups(z):
+    step = up(-(-z.fields // 4), 8)
+    return [(lo, min(step, z.fields - lo)) for lo in range(0, z.fields, step)]
+
+
+def merge_rows(z, chunk, f_ref, o_ref, first, count):
+    lo, hi = z.chunks[chunk]
+    for r in range(lo, hi):
+        o_ref[pl.ds(first * z.rows + r, count, stride=z.rows), :] = f_ref[pl.ds(first * (hi - lo) + r - lo, count, stride=hi - lo), :]
+
+
+def merge0_kernel(z, part, rest, mate, inc, par, o_ref, f_ref):
+    assemble(f_ref, part, rest, mate, par, inc)
+    merge_rows(z, 0, f_ref, o_ref, 0, z.fields)
+
+
+def merge1_kernel(z, part, rest, mate, inc, par, o_in, o_hbm, o_ref, f_ref, sems):
+    assemble(f_ref, part, rest, mate, par, inc)
+    copies = []
+    for k, (first, count) in enumerate(groups(z)):
+        merge_rows(z, 1, f_ref, o_ref, first, count)
+        place = pl.ds(first * z.rows, count * z.rows)
+        copies.append(pltpu.make_async_copy(o_ref.at[place, :], o_hbm.at[place, :], sems.at[k]))
+        copies[-1].start()
+    for copy in copies:
+        copy.wait()
 
 
 VMEM = pl.BlockSpec(memory_space=pltpu.VMEM)
@@ -267,27 +318,49 @@
         )(*ins)
         return res[0]
 
-    def later(self, x, w2, sum0, sum1):
+    def early(self, x, w2, scan):
         z = self.z
         self.x = x
-        self.fixed[1] = pltpu.with_memory_space_constraint(w2, pltpu.HBM)
-        ins = [x, sum0, sum1, *self.fixed]
-        outs = [self.chunk_shape(0), shape(*w2.shape, dtype=BF16)] + self.state
-        specs = [VMEM] * 4 + [HBM] + [VMEM] * 3
+        w1s, _, _, bias, par = self.fixed
+        ins = [x, *scan, w1s, pltpu.with_memory_space_constraint(w2, pltpu.HBM), bias, par]
+        outs = [shape(*w2.shape, dtype=BF16)] + self.state
         res = pl.pallas_call(
-            lambda *refs: later_kernel(z, *refs), out_shape=outs, in_specs=specs, out_specs=[VMEM] * len(outs),
-            scratch_shapes=[pltpu.SemaphoreType.DMA],
-            compiler_params=params(), cost_estimate=cost(z, 0.7), name="later",
+            lambda *refs: early_kernel(z, *refs), out_shape=outs, in_specs=[VMEM] * 5 + [HBM] + [VMEM] * 2,
+            out_specs=[VMEM] * len(outs),
+            scratch_shapes=[pltpu.VMEM(self.chunk_shape(0).shape, F32), pltpu.SemaphoreType.DMA],
+            compiler_params=params(), cost_estimate=cost(z, 0.2), name="early",
         )(*ins)
-        self.fixed[1] = res[1]
-        return res[0], list(res[2:])
-
-    def merge(self, a, b):
+        self.fixed[1] = res[0]
+        return list(res[1:])
+
+    def later(self, scan, state):
+        z = self.z
+        ins = [self.x, *scan, *self.fixed, *state]
+        outs = [self.chunk_shape(0)] + self.state
+        res = pl.pallas_call(
+            lambda *refs: later_kernel(z, *refs), out_shape=outs, in_specs=[VMEM] * len(ins), out_specs=[VMEM] * len(outs),
+            input_output_aliases={len(ins) - 3 + k: 1 + k for k in range(3)},
+            scratch_shapes=[pltpu.VMEM(self.chunk_shape(1).shape, F32)],
+            compiler_params=params(), cost_estimate=cost(z, 0.5), name="later",
+        )(*ins)
+        return res[0], list(res[1:])
+
+    def merge0(self, scan, inc):
         z = self.z
         return pl.pallas_call(
-            lambda *refs: merge_kernel(z, *refs), out_shape=shape(z.fields * z.rows, z.cols),
-            in_specs=[VMEM, VMEM], out_specs=VMEM, compiler_params=params(), name="merge",
-        )(a, b)
+            lambda *refs: merge0_kernel(z, *refs), out_shape=shape(z.fields * z.rows, z.cols),
+            in_specs=[VMEM] * 5, out_specs=VMEM, scratch_shapes=[pltpu.VMEM(self.chunk_shape(0).shape, F32)],
+            compiler_params=params(), name="merge0",
+        )(*scan, inc, self.fixed[4])
+
+    def merge1(self, scan, inc, out):
+        z = self.z
+        return pl.pallas_call(
+            lambda *refs: merge1_kernel(z, *refs), out_shape=[shape(*out.shape), shape(*out.shape)],
+            in_specs=[VMEM] * 6, out_specs=[HBM, VMEM], input_output_aliases={5: 1},
+            scratch_shapes=[pltpu.VMEM(self.chunk_shape(1).shape, F32), pltpu.SemaphoreType.DMA((len(groups(z)),))],
+            compiler_params=params(), name="merge1",
+        )(*scan, inc, self.fixed[4], out)[0]
 
 
 def swap(value, step):
@@ -307,16 +380,18 @@
     length = increment.shape[0]
     half = up(length // 2, 8)
     quarter = up(half // 2, 8)
-    core = owner & 1
     side = (owner >> 1) & 1
     mate = swap(increment, 1)
     pair = increment + mate
     own = lax.dynamic_slice(pair, (places[0], 0), (quarter, pair.shape[1]), allow_negative_indices=False)
     theirs = lax.dynamic_slice(pair, (places[1], 0), (quarter, pair.shape[1]), allow_negative_indices=False)
     got = swap(theirs, 2)
-    total = own + got
-    before = jnp.zeros_like(total)
-    for k in range(2, owners.bit_length() - 1):
+    near = swap(own, 4)
+    cross = swap(theirs, 6)
+    below = near + cross
+    total = own + got + below
+    before = jnp.where((owner & 4) != 0, below, 0.0)
+    for k in range(3, owners.bit_length() - 1):
         far = swap(total, 1 << k)
         before = before + jnp.where((owner & (1 << k)) != 0, far, 0.0)
         total = total + far
@@ -326,10 +401,7 @@
     high = jnp.where(side == 0, back, here)
     part = jnp.concatenate([low[: half - quarter], high], axis=0)
     rest = swap(part, 1)
-    low = jnp.where(core == 0, part, rest)
-    high = jnp.where(core == 0, rest, part)
-    full = jnp.concatenate([low[: length - half], high], axis=0)
-    return full + jnp.where(core == 1, mate, 0.0)
+    return part, rest, mate
 
 
 def shards(states, slab_steps, offset, log_sigma, step_size, w_in, w_mid, w_out, embed):
@@ -345,11 +417,13 @@
             inc0, state = program.open(x, slab_steps, offset, where, (*places[0], *places[1]), log_sigma, step_size, embed.reshape(-1, cols),
                                        w_in.transpose(0, 2, 1), w_mid, w_out)
         else:
-            inc0, state = program.later(x, w_mid, sum0, sum1)
+            state = program.early(x, w_mid, scan0)
+            inc0, state = program.later(scan1, state)
         inc1 = program.close(state)
-        sum0 = earlier_sum(inc0, owner, places[0])
-        sum1 = earlier_sum(inc1, owner, places[1])
-    return program.merge(sum0 + inc0, sum1 + inc1).reshape(states.shape)
+        scan0 = earlier_sum(inc0, owner, places[0])
+        scan1 = earlier_sum(inc1, owner, places[1])
+    out = program.merge0(scan0, inc0)
+    return program.merge1(scan1, inc1, out).reshape(states.shape)
 
 
 def solution(mesh):

time: 66.7 us -> 65.7 us (0.985)
  waiting for transfers between devices: 20.9 us -> 15.9 us
  starting transfers between devices: 28.3 us -> 31.7 us
  Pallas kernels: 15 us -> 15.9 us
    ppermute x24 -> x28, waiting for transfers between devices: 20.9 us -> 15.9 us  [swap(): lax.ppermute(value, 'tm', [(j, j ^ step) for j in range(lax.axis_size('tm...]
    ppermute x24 -> x28, starting transfers between devices: 28.3 us -> 31.7 us  [swap(): lax.ppermute(value, 'tm', [(j, j ^ step) for j in range(lax.axis_size('tm...]
    pallas_call x1 -> x3, Pallas kernels: 0.85 us -> 2.96 us  [the longest x1 1.98 us: early(): pl.pallas_call(lambda *refs: early_kernel(z, *refs), out_shape=outs, in_s...]
    pallas_call x1, Pallas kernels: 4.37 us -> 3.17 us  [later(): pl.pallas_call(lambda *refs: later_kernel(z, *refs), out_shape=outs, in_s...]
  transfers between devices with their start and end apart: 24 -> 28, of which waited for: 18 -> 12; matrix products, arithmetic and copies ran while one was open for 1% -> 1% of each run, Pallas kernels for 0% -> 10%
where the time goes in v3:
time: 65.7 us; the launch traced here: 65.5 us
  starting transfers between devices  31.7 us (48%)
  Pallas kernels  15.9 us (24%)
  waiting for transfers between devices  15.9 us (24%)
  between operations  1.56 us (2%)
    ppermute x28, starting transfers between devices, swap(): lax.ppermute(value, 'tm', [(j, j ^ step) for j in range(lax.axis_size('tm...  31.7 us
    ppermute x28, waiting for transfers between devices, swap(): lax.ppermute(value, 'tm', [(j, j ^ step) for j in range(lax.axis_size('tm...  15.9 us
    pallas_call x1, Pallas kernels, open(): pl.pallas_call(lambda *refs: open_kernel(z, *refs), out_shape=outs, in_sp...  5.27 us
    pallas_call x2, Pallas kernels, close(): pl.pallas_call(lambda *refs: close_kernel(z, *refs), out_shape=outs, in_s...  4.47 us
    pallas_call x1, Pallas kernels, later(): pl.pallas_call(lambda *refs: later_kernel(z, *refs), out_shape=outs, in_s...  3.17 us
    pallas_call x1, Pallas kernels, early(): pl.pallas_call(lambda *refs: early_kernel(z, *refs), out_shape=outs, in_s...  1.98 us
  transfers between devices with their start and end apart: 28, of which 12 were waited for; matrix products, arithmetic and copies ran while one was open for 1% of the time, Pallas kernels for 10%

profile of v3, /device:TPU:0, one launch (start us, length us, event | category | flops | bytes accessed | tf_op | source)
XLA Modules:
  0.0 65.5 jit_solution(193650847444067293)
XLA Ops:
  1.3 5.3 %open.1 = (f32[504,128]{1,0:T(8,128)S(1)}, f32[1008,128]{1,0:T(8,128)S(1)}, bf16[3,256,256]{2,1,0:T(8,128)(2,1)S(1)}, bf16[9,256,256]{2,1,0:T(8,128)(2,1)S(1)}, ...) custom-call(f32[1008,128]{1,0:T(8,128)} %bitcast.7, ...), custom_call_target="tpu_custom_call" | custom-call | flops 2100717184 | bytes 1048576 | tf_op jit(solution)/shard_map/open/pallas_call | solution.py:298
  7.1 2.2 %close.2 = (f32[504,128]{1,0:T(8,128)S(1)}, bf16[256,1792]{1,0:T(8,128)(2,1)S(1)}, bf16[3,256,1792]{2,1,0:T(8,128)(2,1)S(1)}, bf16[256,1792]{1,0:T(8,128)(2,1)S(1)}) custom-call(f32[1008,128]{1,0:T(8,128)S(1)} %get-tuple-element.32.refs_0_, ...), custom_call_target="tpu_custom_call", output_to_operand_aliasing={{1}: (6, {}), {2}: (7, {}), {3}: (8, {})} | custom-call | flops 900307328 | bytes 1048576 | tf_op jit(solution)/shard_map/close/pallas_call | solution.py:314
  9.6 4.1 %collective-permute-start.2 = (f32[128,128]{1,0:T(8,128)S(1)}, f32[128,128]{1,0:T(8,128)S(1)}, u32[]{:S(2)}, u32[]{:S(2)}) collective-permute-start(f32[128,128]{1,0:T(8,128)S(1)} %get-tuple-element.61), channel_id=1, source_target_pairs={{0,6},{1,7},{2,4},{3,5},{4,2},{5,3},{6,0},{7,1},{8,14},{9,15},{10,... | collective-permute-start | bytes 196616 | tf_op jit(solution)/shard_map/ppermute | solution.py:367
  14.3 1.9 %collective-permute-start.10 = (f32[128,128]{1,0:T(8,128)S(1)}, f32[128,128]{1,0:T(8,128)S(1)}, u32[]{:S(2)}, u32[]{:S(2)}) collective-permute-start(f32[128,128]{1,0:T(8,128)S(1)} %get-tuple-element.59), channel_id=1, source_target_pairs={{0,2},{1,3},{2,0},{3,1},{4,6},{5,7},{6,4},{7,5},{8,10},{9,11},{10,... | collective-permute-start | bytes 196616 | tf_op jit(solution)/shard_map/ppermute | solution.py:367
  16.2 1.5 %collective-permute-start.9 = (f32[128,128]{1,0:T(8,128)S(1)}, f32[128,128]{1,0:T(8,128)S(1)}, u32[]{:S(2)}, u32[]{:S(2)}) collective-permute-start(f32[128,128]{1,0:T(8,128)S(1)} %get-tuple-element.59), channel_id=1, source_target_pairs={{0,6},{1,7},{2,4},{3,5},{4,2},{5,3},{6,0},{7,1},{8,14},{9,15},{10,... | collective-permute-start | bytes 196616 | tf_op jit(solution)/shard_map/ppermute | solution.py:367
  17.7 1.3 %collective-permute-done.1 = f32[128,128]{1,0:T(8,128)S(1)} collective-permute-done((f32[128,128]{1,0:T(8,128)S(1)}, f32[128,128]{1,0:T(8,128)S(1)}, u32[]{:S(2)}, u32[]{:S(2)}) %collective-permute-start.1) | collective-permute-done | bytes 65568 | tf_op jit(solution)/shard_map/ppermute | solution.py:367
  19.1 2.7 %collective-permute-start.4 = (f32[128,128]{1,0:T(8,128)S(1)}, f32[128,128]{1,0:T(8,128)S(1)}, u32[]{:S(2)}, u32[]{:S(2)}) collective-permute-start(f32[128,128]{1,0:T(8,128)S(1)} %add_add_fusion.3), channel_id=1, source_target_pairs={{0,8},{1,9},{2,10},{3,11},{4,12},{5,13},{6,14},{7,15},{8,0},{9,1},... | collective-permute-start | bytes 196616 | tf_op jit(solution)/shard_map/ppermute | solution.py:367
  21.8 1.5 %collective-permute-done.8 = f32[128,128]{1,0:T(8,128)S(1)} collective-permute-done((f32[128,128]{1,0:T(8,128)S(1)}, f32[128,128]{1,0:T(8,128)S(1)}, u32[]{:S(2)}, u32[]{:S(2)}) %collective-permute-start.8) | collective-permute-done | bytes 65568 | tf_op jit(solution)/shard_map/ppermute | solution.py:367
  23.3 3.3 %collective-permute-start.11 = (f32[128,128]{1,0:T(8,128)S(1)}, f32[128,128]{1,0:T(8,128)S(1)}, u32[]{:S(2)}, u32[]{:S(2)}) collective-permute-start(f32[128,128]{1,0:T(8,128)S(1)} %add_add_fusion.2), channel_id=1, source_target_pairs={{0,8},{1,9},{2,10},{3,11},{4,12},{5,13},{6,14},{7,15},{8,0},{9,1},... | collective-permute-start | bytes 196616 | tf_op jit(solution)/shard_map/ppermute | solution.py:367
  26.7 1.2 %collective-permute-start.5 = (f32[128,128]{1,0:T(8,128)S(1)}, f32[128,128]{1,0:T(8,128)S(1)}, u32[]{:S(2)}, u32[]{:S(2)}) collective-permute-start(f32[128,128]{1,0:T(8,128)S(1)} %get-tuple-element.53), channel_id=1, source_target_pairs={{0,2},{1,3},{2,0},{3,1},{4,6},{5,7},{6,4},{7,5},{8,10},{9,11},{10,... | collective-permute-start | bytes 196616 | tf_op jit(solution)/shard_map/ppermute | solution.py:367
  27.9 1.3 %collective-permute-done.11 = f32[128,128]{1,0:T(8,128)S(1)} collective-permute-done((f32[128,128]{1,0:T(8,128)S(1)}, f32[128,128]{1,0:T(8,128)S(1)}, u32[]{:S(2)}, u32[]{:S(2)}) %collective-permute-start.11) | collective-permute-done | bytes 65568 | tf_op jit(solution)/shard_map/ppermute | solution.py:367
  29.2 1.7 %collective-permute-start.12 = (f32[128,128]{1,0:T(8,128)S(1)}, f32[128,128]{1,0:T(8,128)S(1)}, u32[]{:S(2)}, u32[]{:S(2)}) collective-permute-start(f32[128,128]{1,0:T(8,128)S(1)} %get-tuple-element.51), channel_id=1, source_target_pairs={{0,2},{1,3},{2,0},{3,1},{4,6},{5,7},{6,4},{7,5},{8,10},{9,11},{10,... | collective-permute-start | bytes 196616 | tf_op jit(solution)/shard_map/ppermute | solution.py:367
  31.1 2.4 %collective-permute-done.12 = f32[128,128]{1,0:T(8,128)S(1)} collective-permute-done((f32[128,128]{1,0:T(8,128)S(1)}, f32[128,128]{1,0:T(8,128)S(1)}, u32[]{:S(2)}, u32[]{:S(2)}) %collective-permute-start.12) | collective-permute-done | bytes 65568 | tf_op jit(solution)/shard_map/ppermute | solution.py:367
  33.7 2.0 %early.1 = (bf16[9,256,256]{2,1,0:T(8,128)(2,1)S(1)}, bf16[256,1792]{1,0:T(8,128)(2,1)S(1)}, bf16[3,256,1792]{2,1,0:T(8,128)(2,1)S(1)}, bf16[256,1792]{1,0:T(8,128)(2,1)S(1)}) custom-call(f32[1008,128]{1,0:T(8,128)S(1)} %bitcast.8, f32[256,128]{1,0:T(8,128)S(1)} %pad_maximum_fusion.refs_1_, f32[256,128]{1,0:T(8,128)S(1)} %collective-permute-done.6.refs_2_, ...), custom_call_target="tpu_custom_call" | custom-call | flops 600204928 | bytes 1048576 | tf_op jit(solution)/shard_map/early/pallas_call | solution.py:327
  35.7 3.2 %later.1 = (f32[504,128]{1,0:T(8,128)S(1)}, bf16[256,1792]{1,0:T(8,128)(2,1)S(1)}, bf16[3,256,1792]{2,1,0:T(8,128)(2,1)S(1)}, bf16[256,1792]{1,0:T(8,128)(2,1)S(1)}) custom-call(f32[1008,128]{1,0:T(8,128)S(1)} %bitcast.9, f32[256,128]{1,0:T(8,128)S(1)} %pad_maximum_fusion.1.refs_1_, ...), custom_call_target="tpu_custom_call", output_to_operand_aliasing={{1}: (9, {}), {2}: (10, {}), {3}: (11, {})} | custom-call | flops 1500512256 | bytes 1048576 | tf_op jit(solution)/shard_map/later/pallas_call | solution.py:340
  39.4 2.2 %close.3 = (f32[504,128]{1,0:T(8,128)S(1)}, bf16[256,1792]{1,0:T(8,128)(2,1)S(1)}, bf16[3,256,1792]{2,1,0:T(8,128)(2,1)S(1)}, bf16[256,1792]{1,0:T(8,128)(2,1)S(1)}) custom-call(f32[1008,128]{1,0:T(8,128)S(1)} %bitcast.10, bf16[3,256,256]{2,1,0:T(8,128)(2,1)S(1)} %get-tuple-element.26.refs_4_.refs_1_, ...), custom_call_target="tpu_custom_call", output_to_operand_aliasing={{1}: (6, {}), {2}: (7, {}), {3}: (8, {})} | custom-call | flops 900307328 | bytes 1048576 | tf_op jit(solution)/shard_map/close/pallas_call | solution.py:314
  41.8 1.2 %collective-permute-start.23 = (f32[128,128]{1,0:T(8,128)S(1)}, f32[128,128]{1,0:T(8,128)S(1)}, u32[]{:S(2)}, u32[]{:S(2)}) collective-permute-start(f32[128,128]{1,0:T(8,128)S(1)} %get-tuple-element.55), channel_id=1, source_target_pairs={{0,6},{1,7},{2,4},{3,5},{4,2},{5,3},{6,0},{7,1},{8,14},{9,15},{10,... | collective-permute-start | bytes 196616 | tf_op jit(solution)/shard_map/ppermute | solution.py:367
  43.6 1.8 %collective-permute-start.22 = (f32[128,128]{1,0:T(8,128)S(1)}, f32[128,128]{1,0:T(8,128)S(1)}, u32[]{:S(2)}, u32[]{:S(2)}) collective-permute-start(f32[128,128]{1,0:T(8,128)S(1)} %get-tuple-element.56), channel_id=1, source_target_pairs={{0,4},{1,5},{2,6},{3,7},{4,0},{5,1},{6,2},{7,3},{8,12},{9,13},{10,... | collective-permute-start | bytes 196616 | tf_op jit(solution)/shard_map/ppermute | solution.py:367
  45.4 1.2 %collective-permute-start.16 = (f32[128,128]{1,0:T(8,128)S(1)}, f32[128,128]{1,0:T(8,128)S(1)}, u32[]{:S(2)}, u32[]{:S(2)}) collective-permute-start(f32[128,128]{1,0:T(8,128)S(1)} %get-tuple-element.57), channel_id=1, source_target_pairs={{0,6},{1,7},{2,4},{3,5},{4,2},{5,3},{6,0},{7,1},{8,14},{9,15},{10,... | collective-permute-start | bytes 196616 | tf_op jit(solution)/shard_map/ppermute | solution.py:367
  46.6 0.6 collective-permute-start.17
  47.2 1.6 %collective-permute-done.22 = f32[128,128]{1,0:T(8,128)S(1)} collective-permute-done((f32[128,128]{1,0:T(8,128)S(1)}, f32[128,128]{1,0:T(8,128)S(1)}, u32[]{:S(2)}, u32[]{:S(2)}) %collective-permute-start.22) | collective-permute-done | bytes 65568 | tf_op jit(solution)/shard_map/ppermute | solution.py:367
  48.8 1.3 %collective-permute-start.15 = (f32[128,128]{1,0:T(8,128)S(1)}, f32[128,128]{1,0:T(8,128)S(1)}, u32[]{:S(2)}, u32[]{:S(2)}) collective-permute-start(f32[128,128]{1,0:T(8,128)S(1)} %get-tuple-element.58), channel_id=1, source_target_pairs={{0,4},{1,5},{2,6},{3,7},{4,0},{5,1},{6,2},{7,3},{8,12},{9,13},{10,... | collective-permute-start | bytes 196616 | tf_op jit(solution)/shard_map/ppermute | solution.py:367
  50.2 2.5 %collective-permute-start.25 = (f32[128,128]{1,0:T(8,128)S(1)}, f32[128,128]{1,0:T(8,128)S(1)}, u32[]{:S(2)}, u32[]{:S(2)}) collective-permute-start(f32[128,128]{1,0:T(8,128)S(1)} %add_add_fusion), channel_id=1, source_target_pairs={{0,8},{1,9},{2,10},{3,11},{4,12},{5,13},{6,14},{7,15},{8,0},{9,1},... | collective-permute-start | bytes 196616 | tf_op jit(solution)/shard_map/ppermute | solution.py:367
  52.7 0.9 %collective-permute-done.15 = f32[128,128]{1,0:T(8,128)S(1)} collective-permute-done((f32[128,128]{1,0:T(8,128)S(1)}, f32[128,128]{1,0:T(8,128)S(1)}, u32[]{:S(2)}, u32[]{:S(2)}) %collective-permute-start.15) | collective-permute-done | bytes 65568 | tf_op jit(solution)/shard_map/ppermute | solution.py:367
  53.6 1.8 %collective-permute-start.18 = (f32[128,128]{1,0:T(8,128)S(1)}, f32[128,128]{1,0:T(8,128)S(1)}, u32[]{:S(2)}, u32[]{:S(2)}) collective-permute-start(f32[128,128]{1,0:T(8,128)S(1)} %add_add_fusion.1), channel_id=1, source_target_pairs={{0,8},{1,9},{2,10},{3,11},{4,12},{5,13},{6,14},{7,15},{8,0},{9,1},... | collective-permute-start | bytes 196616 | tf_op jit(solution)/shard_map/ppermute | solution.py:367
  55.3 2.0 %collective-permute-done.25 = f32[128,128]{1,0:T(8,128)S(1)} collective-permute-done((f32[128,128]{1,0:T(8,128)S(1)}, f32[128,128]{1,0:T(8,128)S(1)}, u32[]{:S(2)}, u32[]{:S(2)}) %collective-permute-start.25) | collective-permute-done | bytes 65568 | tf_op jit(solution)/shard_map/ppermute | solution.py:367
  57.3 1.2 %collective-permute-start.26 = (f32[128,128]{1,0:T(8,128)S(1)}, f32[128,128]{1,0:T(8,128)S(1)}, u32[]{:S(2)}, u32[]{:S(2)}) collective-permute-start(f32[128,128]{1,0:T(8,128)S(1)} %get-tuple-element.47), channel_id=1, source_target_pairs={{0,2},{1,3},{2,0},{3,1},{4,6},{5,7},{6,4},{7,5},{8,10},{9,11},{10,... | collective-permute-start | bytes 196616 | tf_op jit(solution)/shard_map/ppermute | solution.py:367
  58.8 1.0 %collective-permute-start.19 = (f32[128,128]{1,0:T(8,128)S(1)}, f32[128,128]{1,0:T(8,128)S(1)}, u32[]{:S(2)}, u32[]{:S(2)}) collective-permute-start(f32[128,128]{1,0:T(8,128)S(1)} %get-tuple-element.49), channel_id=1, source_target_pairs={{0,2},{1,3},{2,0},{3,1},{4,6},{5,7},{6,4},{7,5},{8,10},{9,11},{10,... | collective-permute-start | bytes 196616 | tf_op jit(solution)/shard_map/ppermute | solution.py:367
  59.8 1.8 %collective-permute-done.26 = f32[128,128]{1,0:T(8,128)S(1)} collective-permute-done((f32[128,128]{1,0:T(8,128)S(1)}, f32[128,128]{1,0:T(8,128)S(1)}, u32[]{:S(2)}, u32[]{:S(2)}) %collective-permute-start.26) | collective-permute-done | bytes 65568 | tf_op jit(solution)/shard_map/ppermute | solution.py:367
  61.8 1.4 %collective-permute-done.19 = f32[128,128]{1,0:T(8,128)S(1)} collective-permute-done((f32[128,128]{1,0:T(8,128)S(1)}, f32[128,128]{1,0:T(8,128)S(1)}, u32[]{:S(2)}, u32[]{:S(2)}) %collective-permute-start.19) | collective-permute-done | bytes 65568 | tf_op jit(solution)/shard_map/ppermute | solution.py:367
  63.4 1.2 %collective-permute-done.20.refs_1_ = f32[256,128]{1,0:T(8,128)S(1)} collective-permute-done((f32[256,128]{1,0:T(8,128)S(1)}, f32[256,128]{1,0:T(8,128)S(1)}, u32[]{:S(2)}, u32[]{:S(2)}) %collective-permute-start.20) | collective-permute-done | bytes 131104 | tf_op jit(solution)/shard_map/ppermute | solution.py:367
  64.6 0.9 %merge1.1 = (f32[1008,128]{1,0:T(8,128)}, f32[1008,128]{1,0:T(8,128)S(1)}) custom-call(f32[256,128]{1,0:T(8,128)S(1)} %pad_maximum_fusion.2.refs_0_, f32[256,128]{1,0:T(8,128)S(1)} %collective-permute-done.20.refs_1_, f32[504,128]{1,0:T(8,128)S(1)} %collective-permute-done.14.refs_2_, ...), custom_call_target="tpu_custom_call", output_to_operand_aliasing={{1}: (5, {})} | custom-call | tf_op jit(solution)/shard_map/merge1/pallas_call | solution.py:358
  (57 shorter events, 3.8 us)
Async XLA Ops:
  6.6 2.9 %collective-permute-start = (f32[504,128]{1,0:T(8,128)S(1)}, f32[504,128]{1,0:T(8,128)S(1)}, u32[]{:S(2)}, u32[]{:S(2)}) collective-permute-start(f32[504,128]{1,0:T(8,128)S(1)} %get-tuple-element.27), channel_id=1, source_target_pairs={{0,1},{1,0},{2,3},{3,2},{4,5},{5,4},{6,7},{7,6},{8,9},{9,8},{10,11... | collective-permute-start | bytes 774152 | tf_op jit(solution)/shard_map/ppermute | solution.py:367
  9.4 24.3 %copy-start = (f32[1,84,12,128]{3,0,2,1:T(1,128)S(1)}, f32[1,84,12,128]{3,0,2,1:T(1,128)}, u32[]{:S(2)}) copy-start(f32[1,84,12,128]{3,0,2,1:T(1,128)} %param.9) | copy-start | bytes 1548292
  9.4 4.9 %collective-permute-start.7 = (f32[504,128]{1,0:T(8,128)S(1)}, f32[504,128]{1,0:T(8,128)S(1)}, u32[]{:S(2)}, u32[]{:S(2)}) collective-permute-start(f32[504,128]{1,0:T(8,128)S(1)} %get-tuple-element.37), channel_id=1, source_target_pairs={{0,1},{1,0},{2,3},{3,2},{4,5},{5,4},{6,7},{7,6},{8,9},{9,8},{10,11... | collective-permute-start | bytes 774152 | tf_op jit(solution)/shard_map/ppermute | solution.py:367
  9.6 9.5 %collective-permute-start.2 = (f32[128,128]{1,0:T(8,128)S(1)}, f32[128,128]{1,0:T(8,128)S(1)}, u32[]{:S(2)}, u32[]{:S(2)}) collective-permute-start(f32[128,128]{1,0:T(8,128)S(1)} %get-tuple-element.61), channel_id=1, source_target_pairs={{0,6},{1,7},{2,4},{3,5},{4,2},{5,3},{6,0},{7,1},{8,14},{9,15},{10,... | collective-permute-start | bytes 196616 | tf_op jit(solution)/shard_map/ppermute | solution.py:367
  13.6 5.4 %collective-permute-start.3 = (f32[128,128]{1,0:T(8,128)S(1)}, f32[128,128]{1,0:T(8,128)S(1)}, u32[]{:S(2)}, u32[]{:S(2)}) collective-permute-start(f32[128,128]{1,0:T(8,128)S(1)} %get-tuple-element.61), channel_id=1, source_target_pairs={{0,2},{1,3},{2,0},{3,1},{4,6},{5,7},{6,4},{7,5},{8,10},{9,11},{10,... | collective-permute-start | bytes 196616 | tf_op jit(solution)/shard_map/ppermute | solution.py:367
  14.1 4.9 %collective-permute-start.1 = (f32[128,128]{1,0:T(8,128)S(1)}, f32[128,128]{1,0:T(8,128)S(1)}, u32[]{:S(2)}, u32[]{:S(2)}) collective-permute-start(f32[128,128]{1,0:T(8,128)S(1)} %get-tuple-element.62), channel_id=1, source_target_pairs={{0,4},{1,5},{2,6},{3,7},{4,0},{5,1},{6,2},{7,3},{8,12},{9,13},{10,... | collective-permute-start | bytes 196616 | tf_op jit(solution)/shard_map/ppermute | solution.py:367
  14.3 7.5 %collective-permute-start.10 = (f32[128,128]{1,0:T(8,128)S(1)}, f32[128,128]{1,0:T(8,128)S(1)}, u32[]{:S(2)}, u32[]{:S(2)}) collective-permute-start(f32[128,128]{1,0:T(8,128)S(1)} %get-tuple-element.59), channel_id=1, source_target_pairs={{0,2},{1,3},{2,0},{3,1},{4,6},{5,7},{6,4},{7,5},{8,10},{9,11},{10,... | collective-permute-start | bytes 196616 | tf_op jit(solution)/shard_map/ppermute | solution.py:367
  16.2 7.1 %collective-permute-start.9 = (f32[128,128]{1,0:T(8,128)S(1)}, f32[128,128]{1,0:T(8,128)S(1)}, u32[]{:S(2)}, u32[]{:S(2)}) collective-permute-start(f32[128,128]{1,0:T(8,128)S(1)} %get-tuple-element.59), channel_id=1, source_target_pairs={{0,6},{1,7},{2,4},{3,5},{4,2},{5,3},{6,0},{7,1},{8,14},{9,15},{10,... | collective-permute-start | bytes 196616 | tf_op jit(solution)/shard_map/ppermute | solution.py:367
  19.0 4.3 %collective-permute-start.8 = (f32[128,128]{1,0:T(8,128)S(1)}, f32[128,128]{1,0:T(8,128)S(1)}, u32[]{:S(2)}, u32[]{:S(2)}) collective-permute-start(f32[128,128]{1,0:T(8,128)S(1)} %get-tuple-element.60), channel_id=1, source_target_pairs={{0,4},{1,5},{2,6},{3,7},{4,0},{5,1},{6,2},{7,3},{8,12},{9,13},{10,... | collective-permute-start | bytes 196616 | tf_op jit(solution)/shard_map/ppermute | solution.py:367
  19.1 7.6 %collective-permute-start.4 = (f32[128,128]{1,0:T(8,128)S(1)}, f32[128,128]{1,0:T(8,128)S(1)}, u32[]{:S(2)}, u32[]{:S(2)}) collective-permute-start(f32[128,128]{1,0:T(8,128)S(1)} %add_add_fusion.3), channel_id=1, source_target_pairs={{0,8},{1,9},{2,10},{3,11},{4,12},{5,13},{6,14},{7,15},{8,0},{9,1},... | collective-permute-start | bytes 196616 | tf_op jit(solution)/shard_map/ppermute | solution.py:367
  23.3 5.9 %collective-permute-start.11 = (f32[128,128]{1,0:T(8,128)S(1)}, f32[128,128]{1,0:T(8,128)S(1)}, u32[]{:S(2)}, u32[]{:S(2)}) collective-permute-start(f32[128,128]{1,0:T(8,128)S(1)} %add_add_fusion.2), channel_id=1, source_target_pairs={{0,8},{1,9},{2,10},{3,11},{4,12},{5,13},{6,14},{7,15},{8,0},{9,1},... | collective-permute-start | bytes 196616 | tf_op jit(solution)/shard_map/ppermute | solution.py:367
  26.7 4.3 %collective-permute-start.5 = (f32[128,128]{1,0:T(8,128)S(1)}, f32[128,128]{1,0:T(8,128)S(1)}, u32[]{:S(2)}, u32[]{:S(2)}) collective-permute-start(f32[128,128]{1,0:T(8,128)S(1)} %get-tuple-element.53), channel_id=1, source_target_pairs={{0,2},{1,3},{2,0},{3,1},{4,6},{5,7},{6,4},{7,5},{8,10},{9,11},{10,... | collective-permute-start | bytes 196616 | tf_op jit(solution)/shard_map/ppermute | solution.py:367
  29.2 4.3 %collective-permute-start.12 = (f32[128,128]{1,0:T(8,128)S(1)}, f32[128,128]{1,0:T(8,128)S(1)}, u32[]{:S(2)}, u32[]{:S(2)}) collective-permute-start(f32[128,128]{1,0:T(8,128)S(1)} %get-tuple-element.51), channel_id=1, source_target_pairs={{0,2},{1,3},{2,0},{3,1},{4,6},{5,7},{6,4},{7,5},{8,10},{9,11},{10,... | collective-permute-start | bytes 196616 | tf_op jit(solution)/shard_map/ppermute | solution.py:367
  31.0 2.6 %collective-permute-start.6 = (f32[256,128]{1,0:T(8,128)S(1)}, f32[256,128]{1,0:T(8,128)S(1)}, u32[]{:S(2)}, u32[]{:S(2)}) collective-permute-start(f32[256,128]{1,0:T(8,128)S(1)} %pad_maximum_fusion.refs_1_), channel_id=1, source_target_pairs={{0,1},{1,0},{2,3},{3,2},{4,5},{5,4},{6,7},{7,6},{8,9},{9,8},{10,11... | collective-permute-start | bytes 393224 | tf_op jit(solution)/shard_map/ppermute | solution.py:367
  33.6 2.1 %collective-permute-start.13 = (f32[256,128]{1,0:T(8,128)S(1)}, f32[256,128]{1,0:T(8,128)S(1)}, u32[]{:S(2)}, u32[]{:S(2)}) collective-permute-start(f32[256,128]{1,0:T(8,128)S(1)} %pad_maximum_fusion.1.refs_1_), channel_id=1, source_target_pairs={{0,1},{1,0},{2,3},{3,2},{4,5},{5,4},{6,7},{7,6},{8,9},{9,8},{10,11... | collective-permute-start | bytes 393224 | tf_op jit(solution)/shard_map/ppermute | solution.py:367
  38.9 2.9 %collective-permute-start.21 = (f32[504,128]{1,0:T(8,128)S(1)}, f32[504,128]{1,0:T(8,128)S(1)}, u32[]{:S(2)}, u32[]{:S(2)}) collective-permute-start(f32[504,128]{1,0:T(8,128)S(1)} %get-tuple-element.45.refs_3_), channel_id=1, source_target_pairs={{0,1},{1,0},{2,3},{3,2},{4,5},{5,4},{6,7},{7,6},{8,9},{9,8},{10,11... | collective-permute-start | bytes 774152 | tf_op jit(solution)/shard_map/ppermute | solution.py:367
  41.6 3.7 %collective-permute-start.14 = (f32[504,128]{1,0:T(8,128)S(1)}, f32[504,128]{1,0:T(8,128)S(1)}, u32[]{:S(2)}, u32[]{:S(2)}) collective-permute-start(f32[504,128]{1,0:T(8,128)S(1)} %get-tuple-element.44.refs_3_), channel_id=1, source_target_pairs={{0,1},{1,0},{2,3},{3,2},{4,5},{5,4},{6,7},{7,6},{8,9},{9,8},{10,11... | collective-permute-start | bytes 774152 | tf_op jit(solution)/shard_map/ppermute | solution.py:367
  41.8 8.4 %collective-permute-start.23 = (f32[128,128]{1,0:T(8,128)S(1)}, f32[128,128]{1,0:T(8,128)S(1)}, u32[]{:S(2)}, u32[]{:S(2)}) collective-permute-start(f32[128,128]{1,0:T(8,128)S(1)} %get-tuple-element.55), channel_id=1, source_target_pairs={{0,6},{1,7},{2,4},{3,5},{4,2},{5,3},{6,0},{7,1},{8,14},{9,15},{10,... | collective-permute-start | bytes 196616 | tf_op jit(solution)/shard_map/ppermute | solution.py:367
  43.0 7.2 %collective-permute-start.24 = (f32[128,128]{1,0:T(8,128)S(1)}, f32[128,128]{1,0:T(8,128)S(1)}, u32[]{:S(2)}, u32[]{:S(2)}) collective-permute-start(f32[128,128]{1,0:T(8,128)S(1)} %get-tuple-element.55), channel_id=1, source_target_pairs={{0,2},{1,3},{2,0},{3,1},{4,6},{5,7},{6,4},{7,5},{8,10},{9,11},{10,... | collective-permute-start | bytes 196616 | tf_op jit(solution)/shard_map/ppermute | solution.py:367
  43.6 5.3 %collective-permute-start.22 = (f32[128,128]{1,0:T(8,128)S(1)}, f32[128,128]{1,0:T(8,128)S(1)}, u32[]{:S(2)}, u32[]{:S(2)}) collective-permute-start(f32[128,128]{1,0:T(8,128)S(1)} %get-tuple-element.56), channel_id=1, source_target_pairs={{0,4},{1,5},{2,6},{3,7},{4,0},{5,1},{6,2},{7,3},{8,12},{9,13},{10,... | collective-permute-start | bytes 196616 | tf_op jit(solution)/shard_map/ppermute | solution.py:367
  45.4 8.1 %collective-permute-start.16 = (f32[128,128]{1,0:T(8,128)S(1)}, f32[128,128]{1,0:T(8,128)S(1)}, u32[]{:S(2)}, u32[]{:S(2)}) collective-permute-start(f32[128,128]{1,0:T(8,128)S(1)} %get-tuple-element.57), channel_id=1, source_target_pairs={{0,6},{1,7},{2,4},{3,5},{4,2},{5,3},{6,0},{7,1},{8,14},{9,15},{10,... | collective-permute-start | bytes 196616 | tf_op jit(solution)/shard_map/ppermute | solution.py:367
  46.6 6.9 %collective-permute-start.17 = (f32[128,128]{1,0:T(8,128)S(1)}, f32[128,128]{1,0:T(8,128)S(1)}, u32[]{:S(2)}, u32[]{:S(2)}) collective-permute-start(f32[128,128]{1,0:T(8,128)S(1)} %get-tuple-element.57), channel_id=1, source_target_pairs={{0,2},{1,3},{2,0},{3,1},{4,6},{5,7},{6,4},{7,5},{8,10},{9,11},{10,... | collective-permute-start | bytes 196616 | tf_op jit(solution)/shard_map/ppermute | solution.py:367
  48.8 4.7 %collective-permute-start.15 = (f32[128,128]{1,0:T(8,128)S(1)}, f32[128,128]{1,0:T(8,128)S(1)}, u32[]{:S(2)}, u32[]{:S(2)}) collective-permute-start(f32[128,128]{1,0:T(8,128)S(1)} %get-tuple-element.58), channel_id=1, source_target_pairs={{0,4},{1,5},{2,6},{3,7},{4,0},{5,1},{6,2},{7,3},{8,12},{9,13},{10,... | collective-permute-start | bytes 196616 | tf_op jit(solution)/shard_map/ppermute | solution.py:367
  50.2 7.1 %collective-permute-start.25 = (f32[128,128]{1,0:T(8,128)S(1)}, f32[128,128]{1,0:T(8,128)S(1)}, u32[]{:S(2)}, u32[]{:S(2)}) collective-permute-start(f32[128,128]{1,0:T(8,128)S(1)} %add_add_fusion), channel_id=1, source_target_pairs={{0,8},{1,9},{2,10},{3,11},{4,12},{5,13},{6,14},{7,15},{8,0},{9,1},... | collective-permute-start | bytes 196616 | tf_op jit(solution)/shard_map/ppermute | solution.py:367
  53.6 5.2 %collective-permute-start.18 = (f32[128,128]{1,0:T(8,128)S(1)}, f32[128,128]{1,0:T(8,128)S(1)}, u32[]{:S(2)}, u32[]{:S(2)}) collective-permute-start(f32[128,128]{1,0:T(8,128)S(1)} %add_add_fusion.1), channel_id=1, source_target_pairs={{0,8},{1,9},{2,10},{3,11},{4,12},{5,13},{6,14},{7,15},{8,0},{9,1},... | collective-permute-start | bytes 196616 | tf_op jit(solution)/shard_map/ppermute | solution.py:367
  57.3 4.3 %collective-permute-start.26 = (f32[128,128]{1,0:T(8,128)S(1)}, f32[128,128]{1,0:T(8,128)S(1)}, u32[]{:S(2)}, u32[]{:S(2)}) collective-permute-start(f32[128,128]{1,0:T(8,128)S(1)} %get-tuple-element.47), channel_id=1, source_target_pairs={{0,2},{1,3},{2,0},{3,1},{4,6},{5,7},{6,4},{7,5},{8,10},{9,11},{10,... | collective-permute-start | bytes 196616 | tf_op jit(solution)/shard_map/ppermute | solution.py:367
  58.8 4.3 %collective-permute-start.19 = (f32[128,128]{1,0:T(8,128)S(1)}, f32[128,128]{1,0:T(8,128)S(1)}, u32[]{:S(2)}, u32[]{:S(2)}) collective-permute-start(f32[128,128]{1,0:T(8,128)S(1)} %get-tuple-element.49), channel_id=1, source_target_pairs={{0,2},{1,3},{2,0},{3,1},{4,6},{5,7},{6,4},{7,5},{8,10},{9,11},{10,... | collective-permute-start | bytes 196616 | tf_op jit(solution)/shard_map/ppermute | solution.py:367
  61.7 1.6 %collective-permute-start.27 = (f32[256,128]{1,0:T(8,128)S(1)}, f32[256,128]{1,0:T(8,128)S(1)}, u32[]{:S(2)}, u32[]{:S(2)}) collective-permute-start(f32[256,128]{1,0:T(8,128)S(1)} %pad_maximum_fusion.3.refs_0_), channel_id=1, source_target_pairs={{0,1},{1,0},{2,3},{3,2},{4,5},{5,4},{6,7},{7,6},{8,9},{9,8},{10,11... | collective-permute-start | bytes 393224 | tf_op jit(solution)/shard_map/ppermute | solution.py:367
  63.2 1.4 %collective-permute-start.20 = (f32[256,128]{1,0:T(8,128)S(1)}, f32[256,128]{1,0:T(8,128)S(1)}, u32[]{:S(2)}, u32[]{:S(2)}) collective-permute-start(f32[256,128]{1,0:T(8,128)S(1)} %pad_maximum_fusion.2.refs_0_), channel_id=1, source_target_pairs={{0,1},{1,0},{2,3},{3,2},{4,5},{5,4},{6,7},{7,6},{8,9},{9,8},{10,11... | collective-permute-start | bytes 393224 | tf_op jit(solution)/shard_map/ppermute | solution.py:367

commit v4 on v3

--- a/solution.py
+++ b/solution.py
@@ -131,7 +131,7 @@
 
 
 def clip(z, cut):
-    return min(cut + 2, z.blocks), min(cut + 1, z.blocks), cut
+    return z.blocks, min(cut + 1, z.blocks), cut
 
 
 def open_kernel(z, x_hbm, step_ref, off_ref, owner_ref, place0, place1, place2, place3, ls_hbm, h_hbm, emb_hbm, w1_hbm, w2_hbm, w3_hbm,
@@ -207,9 +207,13 @@
     f_ref[cut:, :] = jnp.where(odd, a, b) + extra[cut:]
 
 
-def early_kernel(z, x_ref, part, rest, mate, w1s, w2_hbm, bias, par, w2, xs, u1, u2, f_ref, sem):
-    copy = pltpu.make_async_copy(w2_hbm, w2, sem)
+def fetch_kernel(src, dst, sem):
+    copy = pltpu.make_async_copy(src, dst, sem)
     copy.start()
+    copy.wait()
+
+
+def early_kernel(z, x_ref, part, rest, mate, w1s, w2, bias, par, xs, u1, u2, f_ref):
     body = Body(z, w1s, w2, None, bias, par, xs, u1, u2)
     body.clear_edges()
     assemble(f_ref, part, rest, mate, par)
@@ -217,9 +221,7 @@
     for r in range(*z.chunks[0]):
         body.load_row(r, jnp.where(is_first, own_rows(z, x_ref, r), get_row(z, 0, f_ref, r)))
     ends = early(z)
-    body.run((0, 0, 0), (ends[0], 0, 0), None)
-    copy.wait()
-    body.run((ends[0], 0, 0), ends, None)
+    body.run((0, 0, 0), ends, None)
 
 
 def later_kernel(z, x_ref, part, rest, mate, w1s, w2, w3s, bias, par, xs_in, u1_in, u2_in, inc_ref, xs, u1, u2, f_ref):
@@ -322,16 +324,21 @@
         z = self.z
         self.x = x
         w1s, _, _, bias, par = self.fixed
-        ins = [x, *scan, w1s, pltpu.with_memory_space_constraint(w2, pltpu.HBM), bias, par]
-        outs = [shape(*w2.shape, dtype=BF16)] + self.state
+        self.fixed[1] = w2
+        ins = [x, *scan, w1s, w2, bias, par]
+        outs = self.state
         res = pl.pallas_call(
-            lambda *refs: early_kernel(z, *refs), out_shape=outs, in_specs=[VMEM] * 5 + [HBM] + [VMEM] * 2,
-            out_specs=[VMEM] * len(outs),
-            scratch_shapes=[pltpu.VMEM(self.chunk_shape(0).shape, F32), pltpu.SemaphoreType.DMA],
+            lambda *refs: early_kernel(z, *refs), out_shape=outs, in_specs=[VMEM] * len(ins), out_specs=[VMEM] * len(outs),
+            scratch_shapes=[pltpu.VMEM(self.chunk_shape(0).shape, F32)],
             compiler_params=params(), cost_estimate=cost(z, 0.2), name="early",
         )(*ins)
-        self.fixed[1] = res[0]
-        return list(res[1:])
+        return list(res)
+
+    def fetch(self, w2):
+        return pl.pallas_call(
+            fetch_kernel, out_shape=shape(*w2.shape, dtype=BF16), in_specs=[HBM], out_specs=VMEM,
+            scratch_shapes=[pltpu.SemaphoreType.DMA], compiler_params=pltpu.CompilerParams(vmem_limit_bytes=1 << 20), name="fetch",
+        )(pltpu.with_memory_space_constraint(w2, pltpu.HBM))
 
     def later(self, scan, state):
         z = self.z
@@ -417,7 +424,8 @@
             inc0, state = program.open(x, slab_steps, offset, where, (*places[0], *places[1]), log_sigma, step_size, embed.reshape(-1, cols),
                                        w_in.transpose(0, 2, 1), w_mid, w_out)
         else:
-            state = program.early(x, w_mid, scan0)
+            near2 = program.fetch(w_mid)
+            state = program.early(x, near2, scan0)
             inc0, state = program.later(scan1, state)
         inc1 = program.close(state)
         scan0 = earlier_sum(inc0, owner, places[0])

time: 65.7 us -> 64.5 us (0.982)
  waiting for transfers between devices: 15.9 us -> 11.8 us
  starting transfers between devices: 31.7 us -> 33.7 us
  Pallas kernels: 15.9 us -> 16.8 us
    ppermute x28, waiting for transfers between devices: 15.9 us -> 11.8 us  [swap(): lax.ppermute(value, 'tm', [(j, j ^ step) for j in range(lax.axis_size('tm...]
    ppermute x28, starting transfers between devices: 31.7 us -> 33.7 us  [swap(): lax.ppermute(value, 'tm', [(j, j ^ step) for j in range(lax.axis_size('tm...]
    pallas_call x0 -> x1, Pallas kernels: none -> 1.28 us  [fetch(): pl.pallas_call(fetch_kernel, out_shape=shape(*w2.shape, dtype=BF16), in_s...]
  transfers between devices with their start and end apart: 28 -> 28, of which waited for: 12 -> 13; matrix products, arithmetic and copies ran while one was open for 1% -> 1% of each run, Pallas kernels for 10% -> 11%
where the time goes in v4:
time: 64.5 us; the launch traced here: 64.3 us
  starting transfers between devices  33.7 us (52%)
  Pallas kernels  16.8 us (26%)
  waiting for transfers between devices  11.8 us (18%)
  between operations  1.58 us (2%)
    ppermute x28, starting transfers between devices, swap(): lax.ppermute(value, 'tm', [(j, j ^ step) for j in range(lax.axis_size('tm...  33.7 us
    ppermute x28, waiting for transfers between devices, swap(): lax.ppermute(value, 'tm', [(j, j ^ step) for j in range(lax.axis_size('tm...  11.8 us
    pallas_call x1, Pallas kernels, open(): pl.pallas_call(lambda *refs: open_kernel(z, *refs), out_shape=outs, in_sp...  5.43 us
    pallas_call x2, Pallas kernels, close(): pl.pallas_call(lambda *refs: close_kernel(z, *refs), out_shape=outs, in_s...  4.31 us
    pallas_call x1, Pallas kernels, later(): pl.pallas_call(lambda *refs: later_kernel(z, *refs), out_shape=outs, in_s...  3.4 us
    pallas_call x1, Pallas kernels, early(): pl.pallas_call(lambda *refs: early_kernel(z, *refs), out_shape=outs, in_s...  1.43 us
  transfers between devices with their start and end apart: 28, of which 13 were waited for; matrix products, arithmetic and copies ran while one was open for 1% of the time, Pallas kernels for 11%

profile of v4, /device:TPU:0, one launch (start us, length us, event | category | flops | bytes accessed | tf_op | source)
XLA Modules:
  0.0 64.3 jit_solution(920026556992480987)
XLA Ops:
  1.3 5.4 %open.1 = (f32[504,128]{1,0:T(8,128)S(1)}, f32[1008,128]{1,0:T(8,128)S(1)}, bf16[3,256,256]{2,1,0:T(8,128)(2,1)S(1)}, bf16[9,256,256]{2,1,0:T(8,128)(2,1)S(1)}, ...) custom-call(f32[1008,128]{1,0:T(8,128)} %bitcast.7, ...), custom_call_target="tpu_custom_call" | custom-call | flops 2100717184 | bytes 1048576 | tf_op jit(solution)/shard_map/open/pallas_call | solution.py:300
  7.3 2.2 %close.2 = (f32[504,128]{1,0:T(8,128)S(1)}, bf16[256,1792]{1,0:T(8,128)(2,1)S(1)}, bf16[3,256,1792]{2,1,0:T(8,128)(2,1)S(1)}, bf16[256,1792]{1,0:T(8,128)(2,1)S(1)}) custom-call(f32[1008,128]{1,0:T(8,128)S(1)} %get-tuple-element.29.refs_0_, ...), custom_call_target="tpu_custom_call", output_to_operand_aliasing={{1}: (6, {}), {2}: (7, {}), {3}: (8, {})} | custom-call | flops 900307328 | bytes 1048576 | tf_op jit(solution)/shard_map/close/pallas_call | solution.py:316
  9.6 3.0 %collective-permute-start.10 = (f32[128,128]{1,0:T(8,128)S(1)}, f32[128,128]{1,0:T(8,128)S(1)}, u32[]{:S(2)}, u32[]{:S(2)}) collective-permute-start(f32[128,128]{1,0:T(8,128)S(1)} %get-tuple-element.57), channel_id=1, source_target_pairs={{0,2},{1,3},{2,0},{3,1},{4,6},{5,7},{6,4},{7,5},{8,10},{9,11},{10,... | collective-permute-start | bytes 196616 | tf_op jit(solution)/shard_map/ppermute | solution.py:374
  12.7 1.5 %collective-permute-start.9 = (f32[128,128]{1,0:T(8,128)S(1)}, f32[128,128]{1,0:T(8,128)S(1)}, u32[]{:S(2)}, u32[]{:S(2)}) collective-permute-start(f32[128,128]{1,0:T(8,128)S(1)} %get-tuple-element.57), channel_id=1, source_target_pairs={{0,6},{1,7},{2,4},{3,5},{4,2},{5,3},{6,0},{7,1},{8,14},{9,15},{10,... | collective-permute-start | bytes 196616 | tf_op jit(solution)/shard_map/ppermute | solution.py:374
  14.3 2.0 %collective-permute-start.3 = (f32[128,128]{1,0:T(8,128)S(1)}, f32[128,128]{1,0:T(8,128)S(1)}, u32[]{:S(2)}, u32[]{:S(2)}) collective-permute-start(f32[128,128]{1,0:T(8,128)S(1)} %get-tuple-element.59), channel_id=1, source_target_pairs={{0,2},{1,3},{2,0},{3,1},{4,6},{5,7},{6,4},{7,5},{8,10},{9,11},{10,... | collective-permute-start | bytes 196616 | tf_op jit(solution)/shard_map/ppermute | solution.py:374
  16.3 1.5 %collective-permute-start.2 = (f32[128,128]{1,0:T(8,128)S(1)}, f32[128,128]{1,0:T(8,128)S(1)}, u32[]{:S(2)}, u32[]{:S(2)}) collective-permute-start(f32[128,128]{1,0:T(8,128)S(1)} %get-tuple-element.59), channel_id=1, source_target_pairs={{0,6},{1,7},{2,4},{3,5},{4,2},{5,3},{6,0},{7,1},{8,14},{9,15},{10,... | collective-permute-start | bytes 196616 | tf_op jit(solution)/shard_map/ppermute | solution.py:374
  17.9 1.2 %collective-permute-done.8 = f32[128,128]{1,0:T(8,128)S(1)} collective-permute-done((f32[128,128]{1,0:T(8,128)S(1)}, f32[128,128]{1,0:T(8,128)S(1)}, u32[]{:S(2)}, u32[]{:S(2)}) %collective-permute-start.8) | collective-permute-done | bytes 65568 | tf_op jit(solution)/shard_map/ppermute | solution.py:374
  19.1 2.8 %collective-permute-start.11 = (f32[128,128]{1,0:T(8,128)S(1)}, f32[128,128]{1,0:T(8,128)S(1)}, u32[]{:S(2)}, u32[]{:S(2)}) collective-permute-start(f32[128,128]{1,0:T(8,128)S(1)} %add_add_fusion.2), channel_id=1, source_target_pairs={{0,8},{1,9},{2,10},{3,11},{4,12},{5,13},{6,14},{7,15},{8,0},{9,1},... | collective-permute-start | bytes 196616 | tf_op jit(solution)/shard_map/ppermute | solution.py:374
  21.8 0.8 %collective-permute-done.1 = f32[128,128]{1,0:T(8,128)S(1)} collective-permute-done((f32[128,128]{1,0:T(8,128)S(1)}, f32[128,128]{1,0:T(8,128)S(1)}, u32[]{:S(2)}, u32[]{:S(2)}) %collective-permute-start.1) | collective-permute-done | bytes 65568 | tf_op jit(solution)/shard_map/ppermute | solution.py:374
  22.7 2.3 %collective-permute-start.4 = (f32[128,128]{1,0:T(8,128)S(1)}, f32[128,128]{1,0:T(8,128)S(1)}, u32[]{:S(2)}, u32[]{:S(2)}) collective-permute-start(f32[128,128]{1,0:T(8,128)S(1)} %add_add_fusion.3), channel_id=1, source_target_pairs={{0,8},{1,9},{2,10},{3,11},{4,12},{5,13},{6,14},{7,15},{8,0},{9,1},... | collective-permute-start | bytes 196616 | tf_op jit(solution)/shard_map/ppermute | solution.py:374
  24.9 1.4 %collective-permute-done.11 = f32[128,128]{1,0:T(8,128)S(1)} collective-permute-done((f32[128,128]{1,0:T(8,128)S(1)}, f32[128,128]{1,0:T(8,128)S(1)}, u32[]{:S(2)}, u32[]{:S(2)}) %collective-permute-start.11) | collective-permute-done | bytes 65568 | tf_op jit(solution)/shard_map/ppermute | solution.py:374
  26.3 1.7 %collective-permute-start.12 = (f32[128,128]{1,0:T(8,128)S(1)}, f32[128,128]{1,0:T(8,128)S(1)}, u32[]{:S(2)}, u32[]{:S(2)}) collective-permute-start(f32[128,128]{1,0:T(8,128)S(1)} %get-tuple-element.49), channel_id=1, source_target_pairs={{0,2},{1,3},{2,0},{3,1},{4,6},{5,7},{6,4},{7,5},{8,10},{9,11},{10,... | collective-permute-start | bytes 196616 | tf_op jit(solution)/shard_map/ppermute | solution.py:374
  28.6 1.4 %collective-permute-start.5 = (f32[128,128]{1,0:T(8,128)S(1)}, f32[128,128]{1,0:T(8,128)S(1)}, u32[]{:S(2)}, u32[]{:S(2)}) collective-permute-start(f32[128,128]{1,0:T(8,128)S(1)} %get-tuple-element.51), channel_id=1, source_target_pairs={{0,2},{1,3},{2,0},{3,1},{4,6},{5,7},{6,4},{7,5},{8,10},{9,11},{10,... | collective-permute-start | bytes 196616 | tf_op jit(solution)/shard_map/ppermute | solution.py:374
  30.1 0.6 collective-permute-done.12
  30.8 2.1 %collective-permute-done.5 = f32[128,128]{1,0:T(8,128)S(1)} collective-permute-done((f32[128,128]{1,0:T(8,128)S(1)}, f32[128,128]{1,0:T(8,128)S(1)}, u32[]{:S(2)}, u32[]{:S(2)}) %collective-permute-start.5) | collective-permute-done | bytes 65568 | tf_op jit(solution)/shard_map/ppermute | solution.py:374
  33.1 1.3 %fetch.1.refs_5_.refs_2_ = bf16[9,256,256]{2,1,0:T(8,128)(2,1)S(1)} custom-call(bf16[9,256,256]{2,1,0:T(8,128)(2,1)} %src.1), custom_call_target="tpu_custom_call" | custom-call | tf_op jit(solution)/shard_map/fetch/pallas_call | solution.py:338
  34.4 1.4 %early.1 = (bf16[256,1792]{1,0:T(8,128)(2,1)S(1)}, bf16[3,256,1792]{2,1,0:T(8,128)(2,1)S(1)}, bf16[256,1792]{1,0:T(8,128)(2,1)S(1)}) custom-call(f32[1008,128]{1,0:T(8,128)S(1)} %bitcast.8, f32[256,128]{1,0:T(8,128)S(1)} %pad_maximum_fusion.1.refs_1_, f32[256,128]{1,0:T(8,128)S(1)} %collective-permute-done.13.refs_2_, ...), custom_call_target="tpu_custom_call" | custom-call | flops 600204928 | bytes 1048576 | tf_op jit(solution)/shard_map/early/pallas_call | solution.py:330
  35.8 3.4 %later.1 = (f32[504,128]{1,0:T(8,128)S(1)}, bf16[256,1792]{1,0:T(8,128)(2,1)S(1)}, bf16[3,256,1792]{2,1,0:T(8,128)(2,1)S(1)}, bf16[256,1792]{1,0:T(8,128)(2,1)S(1)}) custom-call(f32[1008,128]{1,0:T(8,128)S(1)} %bitcast.9, f32[256,128]{1,0:T(8,128)S(1)} %pad_maximum_fusion.refs_1_, ...), custom_call_target="tpu_custom_call", output_to_operand_aliasing={{1}: (9, {}), {2}: (10, {}), {3}: (11, {})} | custom-call | flops 1500512256 | bytes 1048576 | tf_op jit(solution)/shard_map/later/pallas_call | solution.py:347
  39.8 2.2 %close.3 = (f32[504,128]{1,0:T(8,128)S(1)}, bf16[256,1792]{1,0:T(8,128)(2,1)S(1)}, bf16[3,256,1792]{2,1,0:T(8,128)(2,1)S(1)}, bf16[256,1792]{1,0:T(8,128)(2,1)S(1)}) custom-call(f32[1008,128]{1,0:T(8,128)S(1)} %bitcast.10, bf16[3,256,256]{2,1,0:T(8,128)(2,1)S(1)} %get-tuple-element.25.refs_1_.refs_4_, ...), custom_call_target="tpu_custom_call", output_to_operand_aliasing={{1}: (6, {}), {2}: (7, {}), {3}: (8, {})} | custom-call | flops 900307328 | bytes 1048576 | tf_op jit(solution)/shard_map/close/pallas_call | solution.py:316
  42.1 1.4 %collective-permute-start.24 = (f32[128,128]{1,0:T(8,128)S(1)}, f32[128,128]{1,0:T(8,128)S(1)}, u32[]{:S(2)}, u32[]{:S(2)}) collective-permute-start(f32[128,128]{1,0:T(8,128)S(1)} %get-tuple-element.53), channel_id=1, source_target_pairs={{0,2},{1,3},{2,0},{3,1},{4,6},{5,7},{6,4},{7,5},{8,10},{9,11},{10,... | collective-permute-start | bytes 196616 | tf_op jit(solution)/shard_map/ppermute | solution.py:374
  43.9 1.7 %collective-permute-start.22 = (f32[128,128]{1,0:T(8,128)S(1)}, f32[128,128]{1,0:T(8,128)S(1)}, u32[]{:S(2)}, u32[]{:S(2)}) collective-permute-start(f32[128,128]{1,0:T(8,128)S(1)} %get-tuple-element.54), channel_id=1, source_target_pairs={{0,4},{1,5},{2,6},{3,7},{4,0},{5,1},{6,2},{7,3},{8,12},{9,13},{10,... | collective-permute-start | bytes 196616 | tf_op jit(solution)/shard_map/ppermute | solution.py:374
  45.7 1.4 %collective-permute-start.17 = (f32[128,128]{1,0:T(8,128)S(1)}, f32[128,128]{1,0:T(8,128)S(1)}, u32[]{:S(2)}, u32[]{:S(2)}) collective-permute-start(f32[128,128]{1,0:T(8,128)S(1)} %get-tuple-element.55), channel_id=1, source_target_pairs={{0,2},{1,3},{2,0},{3,1},{4,6},{5,7},{6,4},{7,5},{8,10},{9,11},{10,... | collective-permute-start | bytes 196616 | tf_op jit(solution)/shard_map/ppermute | solution.py:374
  47.5 1.7 %collective-permute-start.15 = (f32[128,128]{1,0:T(8,128)S(1)}, f32[128,128]{1,0:T(8,128)S(1)}, u32[]{:S(2)}, u32[]{:S(2)}) collective-permute-start(f32[128,128]{1,0:T(8,128)S(1)} %get-tuple-element.56), channel_id=1, source_target_pairs={{0,4},{1,5},{2,6},{3,7},{4,0},{5,1},{6,2},{7,3},{8,12},{9,13},{10,... | collective-permute-start | bytes 196616 | tf_op jit(solution)/shard_map/ppermute | solution.py:374
  49.5 2.6 %collective-permute-start.25 = (f32[128,128]{1,0:T(8,128)S(1)}, f32[128,128]{1,0:T(8,128)S(1)}, u32[]{:S(2)}, u32[]{:S(2)}) collective-permute-start(f32[128,128]{1,0:T(8,128)S(1)} %add_add_fusion), channel_id=1, source_target_pairs={{0,8},{1,9},{2,10},{3,11},{4,12},{5,13},{6,14},{7,15},{8,0},{9,1},... | collective-permute-start | bytes 196616 | tf_op jit(solution)/shard_map/ppermute | solution.py:374
  52.3 3.0 %collective-permute-start.18 = (f32[128,128]{1,0:T(8,128)S(1)}, f32[128,128]{1,0:T(8,128)S(1)}, u32[]{:S(2)}, u32[]{:S(2)}) collective-permute-start(f32[128,128]{1,0:T(8,128)S(1)} %add_add_fusion.1), channel_id=1, source_target_pairs={{0,8},{1,9},{2,10},{3,11},{4,12},{5,13},{6,14},{7,15},{8,0},{9,1},... | collective-permute-start | bytes 196616 | tf_op jit(solution)/shard_map/ppermute | solution.py:374
  55.4 1.5 %collective-permute-start.26 = (f32[128,128]{1,0:T(8,128)S(1)}, f32[128,128]{1,0:T(8,128)S(1)}, u32[]{:S(2)}, u32[]{:S(2)}) collective-permute-start(f32[128,128]{1,0:T(8,128)S(1)} %get-tuple-element.45), channel_id=1, source_target_pairs={{0,2},{1,3},{2,0},{3,1},{4,6},{5,7},{6,4},{7,5},{8,10},{9,11},{10,... | collective-permute-start | bytes 196616 | tf_op jit(solution)/shard_map/ppermute | solution.py:374
  56.9 0.7 %collective-permute-done.18 = f32[128,128]{1,0:T(8,128)S(1)} collective-permute-done((f32[128,128]{1,0:T(8,128)S(1)}, f32[128,128]{1,0:T(8,128)S(1)}, u32[]{:S(2)}, u32[]{:S(2)}) %collective-permute-start.18) | collective-permute-done | bytes 65568 | tf_op jit(solution)/shard_map/ppermute | solution.py:374
  57.6 1.5 %collective-permute-start.19 = (f32[128,128]{1,0:T(8,128)S(1)}, f32[128,128]{1,0:T(8,128)S(1)}, u32[]{:S(2)}, u32[]{:S(2)}) collective-permute-start(f32[128,128]{1,0:T(8,128)S(1)} %get-tuple-element.47), channel_id=1, source_target_pairs={{0,2},{1,3},{2,0},{3,1},{4,6},{5,7},{6,4},{7,5},{8,10},{9,11},{10,... | collective-permute-start | bytes 196616 | tf_op jit(solution)/shard_map/ppermute | solution.py:374
  59.1 1.0 %collective-permute-done.26 = f32[128,128]{1,0:T(8,128)S(1)} collective-permute-done((f32[128,128]{1,0:T(8,128)S(1)}, f32[128,128]{1,0:T(8,128)S(1)}, u32[]{:S(2)}, u32[]{:S(2)}) %collective-permute-start.26) | collective-permute-done | bytes 65568 | tf_op jit(solution)/shard_map/ppermute | solution.py:374
  60.2 1.8 %collective-permute-done.19 = f32[128,128]{1,0:T(8,128)S(1)} collective-permute-done((f32[128,128]{1,0:T(8,128)S(1)}, f32[128,128]{1,0:T(8,128)S(1)}, u32[]{:S(2)}, u32[]{:S(2)}) %collective-permute-start.19) | collective-permute-done | bytes 65568 | tf_op jit(solution)/shard_map/ppermute | solution.py:374
  62.2 1.2 %collective-permute-done.20.refs_1_ = f32[256,128]{1,0:T(8,128)S(1)} collective-permute-done((f32[256,128]{1,0:T(8,128)S(1)}, f32[256,128]{1,0:T(8,128)S(1)}, u32[]{:S(2)}, u32[]{:S(2)}) %collective-permute-start.20) | collective-permute-done | bytes 131104 | tf_op jit(solution)/shard_map/ppermute | solution.py:374
  63.4 0.9 %merge1.1 = (f32[1008,128]{1,0:T(8,128)}, f32[1008,128]{1,0:T(8,128)S(1)}) custom-call(f32[256,128]{1,0:T(8,128)S(1)} %pad_maximum_fusion.2.refs_0_, f32[256,128]{1,0:T(8,128)S(1)} %collective-permute-done.20.refs_1_, f32[504,128]{1,0:T(8,128)S(1)} %collective-permute-done.14.refs_2_, ...), custom_call_target="tpu_custom_call", output_to_operand_aliasing={{1}: (5, {})} | custom-call | tf_op jit(solution)/shard_map/merge1/pallas_call | solution.py:365
  (58 shorter events, 4.0 us)
Async XLA Ops:
  6.7 2.8 %collective-permute-start.7 = (f32[504,128]{1,0:T(8,128)S(1)}, f32[504,128]{1,0:T(8,128)S(1)}, u32[]{:S(2)}, u32[]{:S(2)}) collective-permute-start(f32[504,128]{1,0:T(8,128)S(1)} %get-tuple-element.35), channel_id=1, source_target_pairs={{0,1},{1,0},{2,3},{3,2},{4,5},{5,4},{6,7},{7,6},{8,9},{9,8},{10,11... | collective-permute-start | bytes 774152 | tf_op jit(solution)/shard_map/ppermute | solution.py:374
  9.5 4.8 %collective-permute-start = (f32[504,128]{1,0:T(8,128)S(1)}, f32[504,128]{1,0:T(8,128)S(1)}, u32[]{:S(2)}, u32[]{:S(2)}) collective-permute-start(f32[504,128]{1,0:T(8,128)S(1)} %get-tuple-element.34), channel_id=1, source_target_pairs={{0,1},{1,0},{2,3},{3,2},{4,5},{5,4},{6,7},{7,6},{8,9},{9,8},{10,11... | collective-permute-start | bytes 774152 | tf_op jit(solution)/shard_map/ppermute | solution.py:374
  9.6 8.2 %collective-permute-start.10 = (f32[128,128]{1,0:T(8,128)S(1)}, f32[128,128]{1,0:T(8,128)S(1)}, u32[]{:S(2)}, u32[]{:S(2)}) collective-permute-start(f32[128,128]{1,0:T(8,128)S(1)} %get-tuple-element.57), channel_id=1, source_target_pairs={{0,2},{1,3},{2,0},{3,1},{4,6},{5,7},{6,4},{7,5},{8,10},{9,11},{10,... | collective-permute-start | bytes 196616 | tf_op jit(solution)/shard_map/ppermute | solution.py:374
  12.7 6.4 %collective-permute-start.9 = (f32[128,128]{1,0:T(8,128)S(1)}, f32[128,128]{1,0:T(8,128)S(1)}, u32[]{:S(2)}, u32[]{:S(2)}) collective-permute-start(f32[128,128]{1,0:T(8,128)S(1)} %get-tuple-element.57), channel_id=1, source_target_pairs={{0,6},{1,7},{2,4},{3,5},{4,2},{5,3},{6,0},{7,1},{8,14},{9,15},{10,... | collective-permute-start | bytes 196616 | tf_op jit(solution)/shard_map/ppermute | solution.py:374
  14.2 4.9 %collective-permute-start.8 = (f32[128,128]{1,0:T(8,128)S(1)}, f32[128,128]{1,0:T(8,128)S(1)}, u32[]{:S(2)}, u32[]{:S(2)}) collective-permute-start(f32[128,128]{1,0:T(8,128)S(1)} %get-tuple-element.58), channel_id=1, source_target_pairs={{0,4},{1,5},{2,6},{3,7},{4,0},{5,1},{6,2},{7,3},{8,12},{9,13},{10,... | collective-permute-start | bytes 196616 | tf_op jit(solution)/shard_map/ppermute | solution.py:374
  14.3 20.1 %copy-start = (f32[1,84,12,128]{3,0,2,1:T(1,128)S(1)}, f32[1,84,12,128]{3,0,2,1:T(1,128)}, u32[]{:S(2)}) copy-start(f32[1,84,12,128]{3,0,2,1:T(1,128)} %param.9) | copy-start | bytes 1548292
  14.3 7.5 %collective-permute-start.3 = (f32[128,128]{1,0:T(8,128)S(1)}, f32[128,128]{1,0:T(8,128)S(1)}, u32[]{:S(2)}, u32[]{:S(2)}) collective-permute-start(f32[128,128]{1,0:T(8,128)S(1)} %get-tuple-element.59), channel_id=1, source_target_pairs={{0,2},{1,3},{2,0},{3,1},{4,6},{5,7},{6,4},{7,5},{8,10},{9,11},{10,... | collective-permute-start | bytes 196616 | tf_op jit(solution)/shard_map/ppermute | solution.py:374
  16.3 6.3 %collective-permute-start.2 = (f32[128,128]{1,0:T(8,128)S(1)}, f32[128,128]{1,0:T(8,128)S(1)}, u32[]{:S(2)}, u32[]{:S(2)}) collective-permute-start(f32[128,128]{1,0:T(8,128)S(1)} %get-tuple-element.59), channel_id=1, source_target_pairs={{0,6},{1,7},{2,4},{3,5},{4,2},{5,3},{6,0},{7,1},{8,14},{9,15},{10,... | collective-permute-start | bytes 196616 | tf_op jit(solution)/shard_map/ppermute | solution.py:374
  17.8 4.8 %collective-permute-start.1 = (f32[128,128]{1,0:T(8,128)S(1)}, f32[128,128]{1,0:T(8,128)S(1)}, u32[]{:S(2)}, u32[]{:S(2)}) collective-permute-start(f32[128,128]{1,0:T(8,128)S(1)} %get-tuple-element.60), channel_id=1, source_target_pairs={{0,4},{1,5},{2,6},{3,7},{4,0},{5,1},{6,2},{7,3},{8,12},{9,13},{10,... | collective-permute-start | bytes 196616 | tf_op jit(solution)/shard_map/ppermute | solution.py:374
  19.1 7.2 %collective-permute-start.11 = (f32[128,128]{1,0:T(8,128)S(1)}, f32[128,128]{1,0:T(8,128)S(1)}, u32[]{:S(2)}, u32[]{:S(2)}) collective-permute-start(f32[128,128]{1,0:T(8,128)S(1)} %add_add_fusion.2), channel_id=1, source_target_pairs={{0,8},{1,9},{2,10},{3,11},{4,12},{5,13},{6,14},{7,15},{8,0},{9,1},... | collective-permute-start | bytes 196616 | tf_op jit(solution)/shard_map/ppermute | solution.py:374
  22.7 5.9 %collective-permute-start.4 = (f32[128,128]{1,0:T(8,128)S(1)}, f32[128,128]{1,0:T(8,128)S(1)}, u32[]{:S(2)}, u32[]{:S(2)}) collective-permute-start(f32[128,128]{1,0:T(8,128)S(1)} %add_add_fusion.3), channel_id=1, source_target_pairs={{0,8},{1,9},{2,10},{3,11},{4,12},{5,13},{6,14},{7,15},{8,0},{9,1},... | collective-permute-start | bytes 196616 | tf_op jit(solution)/shard_map/ppermute | solution.py:374
  26.3 4.3 %collective-permute-start.12 = (f32[128,128]{1,0:T(8,128)S(1)}, f32[128,128]{1,0:T(8,128)S(1)}, u32[]{:S(2)}, u32[]{:S(2)}) collective-permute-start(f32[128,128]{1,0:T(8,128)S(1)} %get-tuple-element.49), channel_id=1, source_target_pairs={{0,2},{1,3},{2,0},{3,1},{4,6},{5,7},{6,4},{7,5},{8,10},{9,11},{10,... | collective-permute-start | bytes 196616 | tf_op jit(solution)/shard_map/ppermute | solution.py:374
  28.6 4.3 %collective-permute-start.5 = (f32[128,128]{1,0:T(8,128)S(1)}, f32[128,128]{1,0:T(8,128)S(1)}, u32[]{:S(2)}, u32[]{:S(2)}) collective-permute-start(f32[128,128]{1,0:T(8,128)S(1)} %get-tuple-element.51), channel_id=1, source_target_pairs={{0,2},{1,3},{2,0},{3,1},{4,6},{5,7},{6,4},{7,5},{8,10},{9,11},{10,... | collective-permute-start | bytes 196616 | tf_op jit(solution)/shard_map/ppermute | solution.py:374
  30.7 3.6 %collective-permute-start.13 = (f32[256,128]{1,0:T(8,128)S(1)}, f32[256,128]{1,0:T(8,128)S(1)}, u32[]{:S(2)}, u32[]{:S(2)}) collective-permute-start(f32[256,128]{1,0:T(8,128)S(1)} %pad_maximum_fusion.1.refs_1_), channel_id=1, source_target_pairs={{0,1},{1,0},{2,3},{3,2},{4,5},{5,4},{6,7},{7,6},{8,9},{9,8},{10,11... | collective-permute-start | bytes 393224 | tf_op jit(solution)/shard_map/ppermute | solution.py:374
  33.0 2.8 %collective-permute-start.6 = (f32[256,128]{1,0:T(8,128)S(1)}, f32[256,128]{1,0:T(8,128)S(1)}, u32[]{:S(2)}, u32[]{:S(2)}) collective-permute-start(f32[256,128]{1,0:T(8,128)S(1)} %pad_maximum_fusion.refs_1_), channel_id=1, source_target_pairs={{0,1},{1,0},{2,3},{3,2},{4,5},{5,4},{6,7},{7,6},{8,9},{9,8},{10,11... | collective-permute-start | bytes 393224 | tf_op jit(solution)/shard_map/ppermute | solution.py:374
  39.2 2.8 %collective-permute-start.21 = (f32[504,128]{1,0:T(8,128)S(1)}, f32[504,128]{1,0:T(8,128)S(1)}, u32[]{:S(2)}, u32[]{:S(2)}) collective-permute-start(f32[504,128]{1,0:T(8,128)S(1)} %get-tuple-element.43.refs_3_), channel_id=1, source_target_pairs={{0,1},{1,0},{2,3},{3,2},{4,5},{5,4},{6,7},{7,6},{8,9},{9,8},{10,11... | collective-permute-start | bytes 774152 | tf_op jit(solution)/shard_map/ppermute | solution.py:374
  41.9 3.7 %collective-permute-start.14 = (f32[504,128]{1,0:T(8,128)S(1)}, f32[504,128]{1,0:T(8,128)S(1)}, u32[]{:S(2)}, u32[]{:S(2)}) collective-permute-start(f32[504,128]{1,0:T(8,128)S(1)} %get-tuple-element.42.refs_3_), channel_id=1, source_target_pairs={{0,1},{1,0},{2,3},{3,2},{4,5},{5,4},{6,7},{7,6},{8,9},{9,8},{10,11... | collective-permute-start | bytes 774152 | tf_op jit(solution)/shard_map/ppermute | solution.py:374
  42.1 5.4 %collective-permute-start.24 = (f32[128,128]{1,0:T(8,128)S(1)}, f32[128,128]{1,0:T(8,128)S(1)}, u32[]{:S(2)}, u32[]{:S(2)}) collective-permute-start(f32[128,128]{1,0:T(8,128)S(1)} %get-tuple-element.53), channel_id=1, source_target_pairs={{0,2},{1,3},{2,0},{3,1},{4,6},{5,7},{6,4},{7,5},{8,10},{9,11},{10,... | collective-permute-start | bytes 196616 | tf_op jit(solution)/shard_map/ppermute | solution.py:374
  43.5 5.9 %collective-permute-start.23 = (f32[128,128]{1,0:T(8,128)S(1)}, f32[128,128]{1,0:T(8,128)S(1)}, u32[]{:S(2)}, u32[]{:S(2)}) collective-permute-start(f32[128,128]{1,0:T(8,128)S(1)} %get-tuple-element.53), channel_id=1, source_target_pairs={{0,6},{1,7},{2,4},{3,5},{4,2},{5,3},{6,0},{7,1},{8,14},{9,15},{10,... | collective-permute-start | bytes 196616 | tf_op jit(solution)/shard_map/ppermute | solution.py:374
  43.9 5.3 %collective-permute-start.22 = (f32[128,128]{1,0:T(8,128)S(1)}, f32[128,128]{1,0:T(8,128)S(1)}, u32[]{:S(2)}, u32[]{:S(2)}) collective-permute-start(f32[128,128]{1,0:T(8,128)S(1)} %get-tuple-element.54), channel_id=1, source_target_pairs={{0,4},{1,5},{2,6},{3,7},{4,0},{5,1},{6,2},{7,3},{8,12},{9,13},{10,... | collective-permute-start | bytes 196616 | tf_op jit(solution)/shard_map/ppermute | solution.py:374
  45.7 6.4 %collective-permute-start.17 = (f32[128,128]{1,0:T(8,128)S(1)}, f32[128,128]{1,0:T(8,128)S(1)}, u32[]{:S(2)}, u32[]{:S(2)}) collective-permute-start(f32[128,128]{1,0:T(8,128)S(1)} %get-tuple-element.55), channel_id=1, source_target_pairs={{0,2},{1,3},{2,0},{3,1},{4,6},{5,7},{6,4},{7,5},{8,10},{9,11},{10,... | collective-permute-start | bytes 196616 | tf_op jit(solution)/shard_map/ppermute | solution.py:374
  47.2 5.2 %collective-permute-start.16 = (f32[128,128]{1,0:T(8,128)S(1)}, f32[128,128]{1,0:T(8,128)S(1)}, u32[]{:S(2)}, u32[]{:S(2)}) collective-permute-start(f32[128,128]{1,0:T(8,128)S(1)} %get-tuple-element.55), channel_id=1, source_target_pairs={{0,6},{1,7},{2,4},{3,5},{4,2},{5,3},{6,0},{7,1},{8,14},{9,15},{10,... | collective-permute-start | bytes 196616 | tf_op jit(solution)/shard_map/ppermute | solution.py:374
  47.5 4.7 %collective-permute-start.15 = (f32[128,128]{1,0:T(8,128)S(1)}, f32[128,128]{1,0:T(8,128)S(1)}, u32[]{:S(2)}, u32[]{:S(2)}) collective-permute-start(f32[128,128]{1,0:T(8,128)S(1)} %get-tuple-element.56), channel_id=1, source_target_pairs={{0,4},{1,5},{2,6},{3,7},{4,0},{5,1},{6,2},{7,3},{8,12},{9,13},{10,... | collective-permute-start | bytes 196616 | tf_op jit(solution)/shard_map/ppermute | solution.py:374
  49.5 5.9 %collective-permute-start.25 = (f32[128,128]{1,0:T(8,128)S(1)}, f32[128,128]{1,0:T(8,128)S(1)}, u32[]{:S(2)}, u32[]{:S(2)}) collective-permute-start(f32[128,128]{1,0:T(8,128)S(1)} %add_add_fusion), channel_id=1, source_target_pairs={{0,8},{1,9},{2,10},{3,11},{4,12},{5,13},{6,14},{7,15},{8,0},{9,1},... | collective-permute-start | bytes 196616 | tf_op jit(solution)/shard_map/ppermute | solution.py:374
  52.3 5.3 %collective-permute-start.18 = (f32[128,128]{1,0:T(8,128)S(1)}, f32[128,128]{1,0:T(8,128)S(1)}, u32[]{:S(2)}, u32[]{:S(2)}) collective-permute-start(f32[128,128]{1,0:T(8,128)S(1)} %add_add_fusion.1), channel_id=1, source_target_pairs={{0,8},{1,9},{2,10},{3,11},{4,12},{5,13},{6,14},{7,15},{8,0},{9,1},... | collective-permute-start | bytes 196616 | tf_op jit(solution)/shard_map/ppermute | solution.py:374
  55.4 4.7 %collective-permute-start.26 = (f32[128,128]{1,0:T(8,128)S(1)}, f32[128,128]{1,0:T(8,128)S(1)}, u32[]{:S(2)}, u32[]{:S(2)}) collective-permute-start(f32[128,128]{1,0:T(8,128)S(1)} %get-tuple-element.45), channel_id=1, source_target_pairs={{0,2},{1,3},{2,0},{3,1},{4,6},{5,7},{6,4},{7,5},{8,10},{9,11},{10,... | collective-permute-start | bytes 196616 | tf_op jit(solution)/shard_map/ppermute | solution.py:374
  57.6 4.3 %collective-permute-start.19 = (f32[128,128]{1,0:T(8,128)S(1)}, f32[128,128]{1,0:T(8,128)S(1)}, u32[]{:S(2)}, u32[]{:S(2)}) collective-permute-start(f32[128,128]{1,0:T(8,128)S(1)} %get-tuple-element.47), channel_id=1, source_target_pairs={{0,2},{1,3},{2,0},{3,1},{4,6},{5,7},{6,4},{7,5},{8,10},{9,11},{10,... | collective-permute-start | bytes 196616 | tf_op jit(solution)/shard_map/ppermute | solution.py:374
  60.1 2.0 %collective-permute-start.27 = (f32[256,128]{1,0:T(8,128)S(1)}, f32[256,128]{1,0:T(8,128)S(1)}, u32[]{:S(2)}, u32[]{:S(2)}) collective-permute-start(f32[256,128]{1,0:T(8,128)S(1)} %pad_maximum_fusion.3.refs_0_), channel_id=1, source_target_pairs={{0,1},{1,0},{2,3},{3,2},{4,5},{5,4},{6,7},{7,6},{8,9},{9,8},{10,11... | collective-permute-start | bytes 393224 | tf_op jit(solution)/shard_map/ppermute | solution.py:374
  62.0 1.4 %collective-permute-start.20 = (f32[256,128]{1,0:T(8,128)S(1)}, f32[256,128]{1,0:T(8,128)S(1)}, u32[]{:S(2)}, u32[]{:S(2)}) collective-permute-start(f32[256,128]{1,0:T(8,128)S(1)} %pad_maximum_fusion.2.refs_0_), channel_id=1, source_target_pairs={{0,1},{1,0},{2,3},{3,2},{4,5},{5,4},{6,7},{7,6},{8,9},{9,8},{10,11... | collective-permute-start | bytes 393224 | tf_op jit(solution)/shard_map/ppermute | solution.py:374
